TPU v7x, 128 devices: a whole 4x4x4 slice. The times are simulated.
128 devices in a mesh: walker: 4 (over x), domain: 32 (over y, z, core).
Axes of the slice: x: 4, y: 4, z: 4, core: 2. Of those that a mesh axis runs over, the one named last changes fastest.
Arguments:
- positions: float32 [8, 3, 32768], P('walker', None, 'domain'), may hold values from -6 to 6
- velocities: float32 [8, 3, 32768], P('walker', None, 'domain'), may hold values from -6 to 6
- species: bfloat16 [32768, 128], P('domain'), may hold values from -6 to 6
- masses: float32 [32768], P('domain'), may hold values from 1 to 4
- send_rows: int32 [32768], P('domain'), may hold values from 0 to 1023
- neighbours: int32 [8, 8, 32768], P('walker', None, 'domain'), may hold values from 0 to 2047
- live_edges: int32 [8, 8, 32768], P('walker', None, 'domain'), may hold values 0 or 1
- w_rad: float32 [8, 128], replicated, may hold values from -2 to 2
- w_first: bfloat16 [128, 128], replicated, may hold values from -0.5 to 0.5
- w_second: bfloat16 [128, 128], replicated, may hold values from -0.5 to 0.5
- w_update: bfloat16 [128, 128], replicated, may hold values from -0.5 to 0.5
- w_out: float32 [128], replicated, may hold values from -0.5 to 0.5
- weights: float32 [8], replicated, may hold values from 0.1 to 1
- bins: int32 [8], replicated, may hold values from 0 to 3
- copy_src: int32 [8], replicated, may hold values from 0 to 7, as said below
Outputs:
- out_positions: float32 [8, 3, 32768], P('walker', None, 'domain')
- out_velocities: float32 [8, 3, 32768], P('walker', None, 'domain')
- new_weights: float32 [8], replicated
Inputs may be any that keep to these rules, and one draw needn't show every extreme that they name: `copy_src`: every walker whose index is a multiple of 2, and the last walker, is copied into at least one slot.
All inputs are finite; a program needn't handle non-finite values. No bound on the sum of `live_edges` on one device may be relied on, other than what follows from the above.
Results may differ from a plain program's by a relative error of at most 0.0028.
Values may be sent and summed in bfloat16 or wider, within the bound.
A program may use at most 192 MiB of HBM per device.

v0:
```python
import math

import jax
import jax.numpy as jnp
from jax import lax
from jax.sharding import PartitionSpec as P

OFFSET = 2.0
CUTOFF = 5.0
STEP = 0.2


def with_halo(cells, sides, width):
    for axis, dim in sides:
        count = lax.axis_size(axis)
        head = lax.slice_in_dim(cells, 0, width, axis=dim)
        tail = lax.slice_in_dim(cells, cells.shape[dim] - width, cells.shape[dim], axis=dim)
        cells = jnp.concatenate(
            [
                lax.ppermute(tail, axis, [(i, (i + 1) % count) for i in range(count)]),
                cells,
                lax.ppermute(head, axis, [((i + 1) % count, i) for i in range(count)]),
            ],
            axis=dim,
        )
    return cells


def edge_geometry(own_pos, ext_pos, nbr_hot, w_rad):
    neighbour_pos = jnp.einsum(
        "xe,sae->xsa", ext_pos, nbr_hot.astype(jnp.float32), precision=lax.Precision.HIGHEST
    )
    displace = neighbour_pos - own_pos[:, None, :]
    distance = jnp.sqrt(jnp.sum(displace * displace, axis=0))
    scaled = distance / CUTOFF
    envelope = jnp.square(jnp.maximum(0.0, 1.0 - scaled * scaled))
    orders = jnp.arange(1, w_rad.shape[0] + 1).astype(jnp.float32)
    basis_vals = jnp.cos(scaled[..., None] * orders * math.pi) * envelope[..., None]
    hidden = jnp.einsum("sak,kc->sac", basis_vals, w_rad, precision=lax.Precision.HIGHEST)
    return (displace, jax.nn.silu(hidden).astype(jnp.bfloat16))


def on_device(
    positions,
    velocities,
    species,
    masses,
    send_rows,
    neighbours,
    live_edges,
    w_rad,
    w_first,
    w_second,
    w_update,
    w_out,
    weights,
    bins,
    copy_src,
):
    walkers, _, atom_count = positions.shape
    halo_rows = send_rows.shape[0] // 2
    ext_count = atom_count + 2 * halo_rows
    offset_vec = jnp.array([OFFSET, 0.0, 0.0], dtype=jnp.float32)[None, :, None]
    send_hot = send_rows[:, None] == jnp.arange(atom_count)[None, :]
    send_float = send_hot.astype(jnp.float32)
    send_half = send_hot.astype(jnp.bfloat16)
    sent_pos = jnp.einsum("wxa,ha->wxh", positions, send_float, precision=lax.Precision.HIGHEST)
    widened = with_halo(sent_pos, (("domain", 2),), halo_rows)
    pos_ext = jnp.concatenate(
        [
            positions,
            widened[..., :halo_rows] - offset_vec,
            widened[..., 3 * halo_rows :] + offset_vec,
        ],
        axis=2,
    )
    sent_species = jnp.dot(send_half, species, preferred_element_type=jnp.float32).astype(
        jnp.bfloat16
    )
    wide_species = with_halo(sent_species, (("domain", 0),), halo_rows)
    species_halo = jnp.concatenate(
        [wide_species[:halo_rows], wide_species[3 * halo_rows :]], axis=0
    )
    species_ext = jnp.concatenate([species, species_halo], axis=0)
    live_float = live_edges.astype(jnp.float32)
    ext_ids = jnp.arange(ext_count)

    def first_pass(inputs):
        own_pos, ext_pos, nbr_index, live_mask = inputs
        nbr_hot = (nbr_index[..., None] == ext_ids).astype(jnp.bfloat16)
        displace, hidden = edge_geometry(own_pos, ext_pos, nbr_hot, w_rad)
        filtered = jnp.einsum("sac,cd->sad", hidden, w_first, preferred_element_type=jnp.float32)
        neighbour_species = jnp.einsum(
            "sae,ec->sac", nbr_hot, species_ext, preferred_element_type=jnp.float32
        )
        messages = filtered * neighbour_species * live_mask[..., None]
        aggregate = jnp.sum(messages, axis=0).astype(jnp.bfloat16)
        updated = jnp.dot(aggregate, w_update, preferred_element_type=jnp.float32)
        features = (species.astype(jnp.float32) + jax.nn.silu(updated)).astype(jnp.bfloat16)
        return (features, hidden, displace, nbr_hot)

    features, hiddens, displaces, nbr_hots = lax.map(
        first_pass, (positions, pos_ext, neighbours, live_float)
    )
    sent_feat = jnp.einsum(
        "ha,wac->whc", send_half, features, preferred_element_type=jnp.float32
    ).astype(jnp.bfloat16)
    wide_feat = with_halo(sent_feat, (("domain", 1),), halo_rows)
    feat_ext = jnp.concatenate(
        [features, wide_feat[:, :halo_rows], wide_feat[:, 3 * halo_rows :]], axis=1
    )

    def second_pass(inputs):
        hidden, displace, own_feat, ext_feat, nbr_hot, live_mask = inputs
        filtered = jnp.einsum("sac,cd->sad", hidden, w_second, preferred_element_type=jnp.float32)
        neighbour_feat = jnp.einsum(
            "sae,ec->sac", nbr_hot, ext_feat, preferred_element_type=jnp.float32
        )
        coupling = (
            jnp.sum(filtered * w_out * own_feat.astype(jnp.float32) * neighbour_feat, axis=-1)
            * live_mask
        )
        pair_force = coupling[None] * displace
        reaction = -jnp.einsum(
            "xsa,sae->xe", pair_force, nbr_hot.astype(jnp.float32), precision=lax.Precision.HIGHEST
        )
        return (jnp.sum(pair_force, axis=1) + reaction[:, :atom_count], reaction[:, atom_count:])

    own_force, halo_force = lax.map(
        second_pass, (hiddens, displaces, features, feat_ext, nbr_hots, live_float)
    )
    wide_back = with_halo(halo_force, (("domain", 2),), halo_rows)
    returned = jnp.concatenate(
        [wide_back[..., :halo_rows], wide_back[..., 3 * halo_rows :]], axis=-1
    )
    forces = own_force + jnp.einsum(
        "wxh,ha->wxa", returned, send_float, precision=lax.Precision.HIGHEST
    )
    vel_step = velocities + STEP * forces / masses
    pos_step = positions + STEP * vel_step
    walker_state = jnp.concatenate([pos_step, vel_step], axis=1)
    walker_rank = lax.axis_index("walker")
    sources = lax.dynamic_slice_in_dim(copy_src, walker_rank * walkers, walkers, 0)
    everything = lax.all_gather(walker_state, "walker", axis=0, tiled=True)
    picked = jnp.take(everything, sources, axis=0)
    src_weight = weights[copy_src]
    src_bin = bins[copy_src]
    same_bin = (src_bin[:, None] == src_bin[None, :]).astype(jnp.float32)
    bin_share = jnp.sum(same_bin * src_weight[None, :], axis=1)
    bin_mass = jnp.sum(
        (src_bin[:, None] == bins[None, :]).astype(jnp.float32) * weights[None, :], axis=1
    )
    new_weights = bin_mass * src_weight / bin_share
    return (picked[:, :3], picked[:, 3:], new_weights)


def solution(mesh):
    in_specs = (
        P("walker", None, "domain"),
        P("walker", None, "domain"),
        P("domain", None),
        P("domain"),
        P("domain"),
        P("walker", None, "domain"),
        P("walker", None, "domain"),
        P(),
        P(),
        P(),
        P(),
        P(),
        P(),
        P(),
        P(),
    )
    out_specs = (P("walker", None, "domain"), P("walker", None, "domain"), P())
    return jax.shard_map(
        on_device, mesh=mesh, in_specs=in_specs, out_specs=out_specs, check_vma=False
    )
```

profile of v0, /device:TPU:0, one launch (start us, length us, event | category | flops | bytes accessed | tf_op | source)
XLA Modules:
  0.0 258.6 jit_solution(1518411431366526045)
XLA Ops:
  0.8 2.8 %fusion.79 = f32[2,3,1024]{2,1,0:T(4,128)S(1)} fusion(s32[1024]{0:T(1024)} %param.24, f32[2,3,1024]{2,0,1:T(2,128)} %param.20), kind=kOutput, calls=%fused_computation.87 | convolution fusion | flops 76546048 | bytes 53248 | tf_op jit(solution)/shard_map/wxa,ha->wxh/dot_general | solution.py:67
  3.7 6.1 %collective-permute-start.1 = (f32[2,3,512]{2,1,0:T(4,128)S(1)}, f32[2,3,512]{2,1,0:T(4,128)S(1)}, u32[]{:S(2)}, u32[]{:S(2)}) collective-permute-start(f32[2,3,512]{2,1,0:T(4,128)S(1)} %get-tuple-element.397), channel_id=1, source_target_pairs={{1,0},{2,1},{3,2},{4,3},{5,4},{6,5},{7,6},{8,7},{9,8},{10,9},{11,1... | collective-permute-start | bytes 36872 | tf_op jit(solution)/shard_map/ppermute | solution.py:22
  9.8 1.8 fusion.78
  11.7 5.1 %collective-permute-start.3 = (bf16[512,128]{1,0:T(8,128)(2,1)S(1)}, bf16[512,128]{1,0:T(8,128)(2,1)S(1)}, u32[]{:S(2)}, u32[]{:S(2)}) collective-permute-start(bf16[512,128]{1,0:T(8,128)(2,1)S(1)} %get-tuple-element.391), channel_id=1, source_target_pairs={{1,0},{2,1},{3,2},{4,3},{5,4},{6,5},{7,6},{8,7},{9,8},{10,9},{11,1... | collective-permute-start | bytes 393224 | tf_op jit(solution)/shard_map/ppermute | solution.py:22
  20.5 126.5 %while.31 = (s32[]{:T(128)}, bf16[2,1024,128]{2,1,0:T(8,128)(2,1)S(1)}, bf16[2,8,1024,128]{3,2,1,0:T(8,128)(2,1)}, f32[2,3,8,1024]{3,1,2,0:T(4,128)S(1)}, bf16[2...) while((s32[]{:T(128)}, ...), condition=%wide.region_3.4_spmd.clone.clone, body=%wide.region_0.3_spmd.clone.clone.sunk | while | flops 5378187264 | bytes 84325632 | solution.py:102
  20.8 30.2 %multiply_reduce_fusion.7 = (f32[8,1024]{1,0:T(8,128)S(1)}, f32[3,8,1024]{2,0,1:T(4,128)S(1)}) fusion(f32[3,1024]{1,0:T(4,128)S(1)} %dynamic-slice_bitcast_fusion.6, s32[8,1024]{1,0:T(8,128)S(1)} %dynamic-slice_bitcast_fusion.7, f32[2,3,2048]{2,1,0:T(4,128)S(1)} %get-tuple-element.604, s32[]{:T(128)} %get-tuple-element.583), kind=kOutput, calls=%fused_computation.60.clone.1 | convolution fusion | flops 620822528 | bytes 212996 | tf_op jit(solution)/shard_map/while/body/eval_jaxpr/xe,sae->xsa/dot_general | solution.py:30
  51.1 8.2 %bitcast_dynamic-update-slice_fusion.6 = (bf16[2,8,1024,128]{3,2,1,0:T(8,128)(2,1)S(1)}, bf16[8,1024,128]{2,1,0:T(8,128)(2,1)S(1)}) fusion(bf16[2,8,1024,128]{3,2,1,0:T(8,128)(2,1)S(1)} %copy-done.2, s32[]{:T(128)} %get-tuple-element.583, f32[8,128]{1,0:T(8,128)S(1)} %get-tuple-element.607, f32[8,1024]{1,0:T(8,128)S(1)} %get-tuple-element.563, ...), kind=kOutput, calls=%fused_computation.44.clone.1 | convolution fusion | flops 106102784 | bytes 4264452 | tf_op jit(solution)/shard_map/while/body/eval_jaxpr/sak,kc->sac/dot_general | solution.py:39
  60.0 12.2 %multiply_reduce_fusion.8 = bf16[1024,128]{1,0:T(8,128)(2,1)S(1)} fusion(f32[8,1024,128]{2,1,0:T(8,128)S(1)} %fusion.141, s32[8,1024]{1,0:T(8,128)S(1)} %dynamic-slice_bitcast_fusion.7, f32[8,1024]{1,0:T(8,128)S(1)} %dynamic-slice_bitcast_fusion.8, bf16[2048,128]{1,0:T(8,128)(2,1)S(1)} %get-tuple-element.609), kind=kOutput, calls=%fused_computation.42.clone.1 | convolution fusion | flops 4314759168 | bytes 5046272 | tf_op jit(solution)/shard_map/while/body/eval_jaxpr/sae,ec->sac/dot_general | solution.py:93
  72.6 11.3 %fusion.142 = bf16[2,8,1024,2048]{3,2,1,0:T(8,128)(2,1)} fusion(bf16[2,8,1024,2048]{3,2,1,0:T(8,128)(2,1)} %get-tuple-element.587, s32[]{:T(128)} %get-tuple-element.583, s32[8,1024]{1,0:T(8,128)S(1)} %dynamic-slice_bitcast_fusion.7), kind=kLoop, calls=%fused_computation.39.clone.1 | loop fusion | flops 33554432 | bytes 33587712 | tf_op jit(solution)/shard_map/while/body/jit(dynamic_update_index_in_dim)/dynamic_update_slice | solution.py:102
  83.9 30.2 %multiply_reduce_fusion.7 = (f32[8,1024]{1,0:T(8,128)S(1)}, f32[3,8,1024]{2,0,1:T(4,128)S(1)}) fusion(f32[3,1024]{1,0:T(4,128)S(1)} %dynamic-slice_bitcast_fusion.6, s32[8,1024]{1,0:T(8,128)S(1)} %dynamic-slice_bitcast_fusion.7, f32[2,3,2048]{2,1,0:T(4,128)S(1)} %get-tuple-element.604, s32[]{:T(128)} %get-tuple-element.583), kind=kOutput, calls=%fused_computation.60.clone.1 | convolution fusion | flops 620822528 | bytes 212996 | tf_op jit(solution)/shard_map/while/body/eval_jaxpr/xe,sae->xsa/dot_general | solution.py:30
  114.2 8.2 %bitcast_dynamic-update-slice_fusion.6 = (bf16[2,8,1024,128]{3,2,1,0:T(8,128)(2,1)S(1)}, bf16[8,1024,128]{2,1,0:T(8,128)(2,1)S(1)}) fusion(bf16[2,8,1024,128]{3,2,1,0:T(8,128)(2,1)S(1)} %copy-done.2, s32[]{:T(128)} %get-tuple-element.583, f32[8,128]{1,0:T(8,128)S(1)} %get-tuple-element.607, f32[8,1024]{1,0:T(8,128)S(1)} %get-tuple-element.563, ...), kind=kOutput, calls=%fused_computation.44.clone.1 | convolution fusion | flops 106102784 | bytes 4264452 | tf_op jit(solution)/shard_map/while/body/eval_jaxpr/sak,kc->sac/dot_general | solution.py:39
  123.2 12.2 %multiply_reduce_fusion.8 = bf16[1024,128]{1,0:T(8,128)(2,1)S(1)} fusion(f32[8,1024,128]{2,1,0:T(8,128)S(1)} %fusion.141, s32[8,1024]{1,0:T(8,128)S(1)} %dynamic-slice_bitcast_fusion.7, f32[8,1024]{1,0:T(8,128)S(1)} %dynamic-slice_bitcast_fusion.8, bf16[2048,128]{1,0:T(8,128)(2,1)S(1)} %get-tuple-element.609), kind=kOutput, calls=%fused_computation.42.clone.1 | convolution fusion | flops 4314759168 | bytes 5046272 | tf_op jit(solution)/shard_map/while/body/eval_jaxpr/sae,ec->sac/dot_general | solution.py:93
  135.7 11.3 %fusion.142 = bf16[2,8,1024,2048]{3,2,1,0:T(8,128)(2,1)} fusion(bf16[2,8,1024,2048]{3,2,1,0:T(8,128)(2,1)} %get-tuple-element.587, s32[]{:T(128)} %get-tuple-element.583, s32[8,1024]{1,0:T(8,128)S(1)} %dynamic-slice_bitcast_fusion.7), kind=kLoop, calls=%fused_computation.39.clone.1 | loop fusion | flops 33554432 | bytes 33587712 | tf_op jit(solution)/shard_map/while/body/jit(dynamic_update_index_in_dim)/dynamic_update_slice | solution.py:102
  148.2 5.1 %collective-permute-start.5 = (bf16[2,512,128]{1,2,0:T(8,128)(2,1)S(1)}, bf16[2,512,128]{1,2,0:T(8,128)(2,1)S(1)}, u32[]{:S(2)}, u32[]{:S(2)}) collective-permute-start(bf16[2,512,128]{1,2,0:T(8,128)(2,1)S(1)} %get-tuple-element.389), channel_id=1, source_target_pairs={{1,0},{2,1},{3,2},{4,3},{5,4},{6,5},{7,6},{8,7},{9,8},{10,9},{11,1... | collective-permute-start | bytes 786440 | tf_op jit(solution)/shard_map/ppermute | solution.py:22
  154.0 3.3 %collective-permute-done.4 = bf16[2,512,128]{1,2,0:T(8,128)(2,1)S(1)} collective-permute-done((bf16[2,512,128]{1,2,0:T(8,128)(2,1)S(1)}, bf16[2,512,128]{1,2,0:T(8,128)(2,1)S(1)}, u32[]{:S(2)}, u32[]{:S(2)}) %collective-permute-start.4) | collective-permute-done | bytes 262176 | tf_op jit(solution)/shard_map/ppermute | solution.py:20
  157.8 78.1 %while.30 = (s32[]{:T(128)}, f32[2,3,1024]{2,1,0:T(4,128)S(1)}, f32[2,3,1024]{2,1,0:T(4,128)S(1)}, bf16[2,8,1024,128]{3,2,1,0:T(8,128)(2,1)}, bf16[128,128]{0,1:...) while((s32[]{:T(128)}, f32[2,3,1024]{2,1,0:T(4,128)S(1)}, ...), condition=%wide.region_7.8_spmd, body=%wide.region_4.7_spmd.sunk | while | flops 5171787776 | bytes 81058936 | solution.py:129
  157.8 4.3 %fusion.131 = f32[8,1024,128]{1,2,0:T(8,128)} fusion(bf16[2,8,1024,128]{3,2,1,0:T(8,128)(2,1)} %get-tuple-element.640, s32[]{:T(128)} %get-tuple-element.625, bf16[128,128]{0,1:T(8,128)(2,1)S(1)} %get-tuple-element.641), kind=kOutput, calls=%fused_computation.13.clone.1 | convolution fusion | flops 268435456 | bytes 6324736 | tf_op jit(solution)/shard_map/while/body/eval_jaxpr/sac,cd->sad/dot_general | solution.py:115
  162.4 17.5 %multiply_reduce_fusion.6 = f32[8,1024]{1,0:T(8,128)S(1)} fusion(f32[8,1024,128]{1,2,0:T(8,128)} %fusion.131, bf16[2,8,1024,2048]{3,2,1,0:T(8,128)(2,1)} %get-tuple-element.644, s32[]{:T(128)} %get-tuple-element.625, f32[1024,128]{0,1:T(8,128)S(1)} %bitcast_convert_fusion.2, f32[128]{0:T(128)S(1)} %get-tuple-element.642, ...), kind=kOutput, calls=%fused_computation.10.clone.1 | convolution fusion | flops 4299153408 | bytes 38831616 | tf_op jit(solution)/shard_map/while/body/eval_jaxpr/sae,ec->sac/dot_general | solution.py:116
  179.9 16.9 %fusion.133 = f32[3,2048]{1,0:T(4,128)S(1)} fusion(bf16[2,8,1024,2048]{3,2,1,0:T(8,128)(2,1)} %get-tuple-element.644, s32[]{:T(128)} %get-tuple-element.625, f32[2,3,8,1024]{3,1,2,0:T(4,128)S(1)} %get-tuple-element.647, f32[8,1024]{1,0:T(8,128)S(1)} %fusion.132), kind=kOutput, calls=%fused_computation.12.clone.1 | convolution fusion | flops 604010496 | bytes 33743872 | tf_op jit(solution)/shard_map/while/body/eval_jaxpr/xsa,sae->xe/dot_general | solution.py:124
  196.9 4.3 %fusion.131 = f32[8,1024,128]{1,2,0:T(8,128)} fusion(bf16[2,8,1024,128]{3,2,1,0:T(8,128)(2,1)} %get-tuple-element.640, s32[]{:T(128)} %get-tuple-element.625, bf16[128,128]{0,1:T(8,128)(2,1)S(1)} %get-tuple-element.641), kind=kOutput, calls=%fused_computation.13.clone.1 | convolution fusion | flops 268435456 | bytes 6324736 | tf_op jit(solution)/shard_map/while/body/eval_jaxpr/sac,cd->sad/dot_general | solution.py:115
  201.4 17.5 %multiply_reduce_fusion.6 = f32[8,1024]{1,0:T(8,128)S(1)} fusion(f32[8,1024,128]{1,2,0:T(8,128)} %fusion.131, bf16[2,8,1024,2048]{3,2,1,0:T(8,128)(2,1)} %get-tuple-element.644, s32[]{:T(128)} %get-tuple-element.625, f32[1024,128]{0,1:T(8,128)S(1)} %bitcast_convert_fusion.2, f32[128]{0:T(128)S(1)} %get-tuple-element.642, ...), kind=kOutput, calls=%fused_computation.10.clone.1 | convolution fusion | flops 4299153408 | bytes 38831616 | tf_op jit(solution)/shard_map/while/body/eval_jaxpr/sae,ec->sac/dot_general | solution.py:116
  219.0 16.9 %fusion.133 = f32[3,2048]{1,0:T(4,128)S(1)} fusion(bf16[2,8,1024,2048]{3,2,1,0:T(8,128)(2,1)} %get-tuple-element.644, s32[]{:T(128)} %get-tuple-element.625, f32[2,3,8,1024]{3,1,2,0:T(4,128)S(1)} %get-tuple-element.647, f32[8,1024]{1,0:T(8,128)S(1)} %fusion.132), kind=kOutput, calls=%fused_computation.12.clone.1 | convolution fusion | flops 604010496 | bytes 33743872 | tf_op jit(solution)/shard_map/while/body/eval_jaxpr/xsa,sae->xe/dot_general | solution.py:124
  236.0 5.1 %collective-permute-start.7 = (f32[2,3,512]{2,1,0:T(4,128)S(1)}, f32[2,3,512]{2,1,0:T(4,128)S(1)}, u32[]{:S(2)}, u32[]{:S(2)}) collective-permute-start(f32[2,3,512]{2,1,0:T(4,128)S(1)} %get-tuple-element.395), channel_id=1, source_target_pairs={{1,0},{2,1},{3,2},{4,3},{5,4},{6,5},{7,6},{8,7},{9,8},{10,9},{11,1... | collective-permute-start | bytes 36872 | tf_op jit(solution)/shard_map/ppermute | solution.py:22
  244.1 12.6 %all_gather.3 = f32[8,6,1024]{2,1,0:T(8,128)S(1)} all-gather(f32[2,6,1024]{2,1,0:T(8,128)S(1)} %pad_maximum_fusion.3), channel_id=1, replica_groups=mesh['walker'=4,'domain'=32] {'walker'}, dimensions={0}, use_global_device_ids=true | all-gather | bytes 245760 | tf_op jit(solution)/shard_map/all_gather | solution.py:144
  (127 shorter events, 13.9 us)
Async XLA Ops:
  0.6 19.6 %copy-start.17 = (f32[3]{0:T(128)S(1)}, f32[3]{0:T(128)}, u32[]{:S(2)}) copy-start(f32[3]{0:T(128)} %constant.104) | copy-start | bytes 40
  0.6 19.7 %copy-start.16 = (f32[3]{0:T(128)S(1)}, f32[3]{0:T(128)}, u32[]{:S(2)}) copy-start(f32[3]{0:T(128)} %constant.99.clone) | copy-start | bytes 40
  0.7 19.4 %copy-start.10 = (f32[2,3,1024]{2,0,1:T(2,128)S(1)}, f32[2,3,1024]{2,0,1:T(2,128)}, u32[]{:S(2)}) copy-start(f32[2,3,1024]{2,0,1:T(2,128)} %param.20) | copy-start | bytes 73732
  0.7 19.8 %copy-start.7 = (bf16[1024,128]{1,0:T(8,128)(2,1)S(1)}, bf16[1024,128]{1,0:T(8,128)(2,1)}, u32[]{:S(2)}) copy-start(bf16[1024,128]{1,0:T(8,128)(2,1)} %param.22) | copy-start | bytes 786436
  0.7 18.7 %copy-start = (f32[8]{0:T(128)S(1)}, f32[8]{0:T(128)}, u32[]{:S(2)}) copy-start(f32[8]{0:T(128)} %param.32) | copy-start | bytes 100
  0.7 19.5 %copy-start.8 = (s32[2,8,1024]{2,1,0:T(8,128)S(1)}, s32[2,8,1024]{2,1,0:T(8,128)}, u32[]{:S(2)}) copy-start(s32[2,8,1024]{2,1,0:T(8,128)} %param.26) | copy-start | bytes 196612
  0.7 19.8 %copy-start.6 = (s32[2,8,1024]{2,1,0:T(8,128)S(1)}, s32[2,8,1024]{2,1,0:T(8,128)}, u32[]{:S(2)}) copy-start(s32[2,8,1024]{2,1,0:T(8,128)} %param.25) | copy-start | bytes 196612
  0.7 19.8 %copy-start.21 = (f32[8,128]{1,0:T(8,128)S(1)}, f32[8,128]{1,0:T(8,128)}, u32[]{:S(2)}) copy-start(f32[8,128]{1,0:T(8,128)} %param.27) | copy-start | bytes 12292
  0.7 19.8 %copy-start.4 = (bf16[128,128]{1,0:T(8,128)(2,1)S(1)}, bf16[128,128]{1,0:T(8,128)(2,1)}, u32[]{:S(2)}) copy-start(bf16[128,128]{1,0:T(8,128)(2,1)} %param.28) | copy-start | bytes 98308
  0.7 19.8 %copy-start.19 = (bf16[128,128]{1,0:T(8,128)(2,1)S(1)}, bf16[128,128]{1,0:T(8,128)(2,1)}, u32[]{:S(2)}) copy-start(bf16[128,128]{1,0:T(8,128)(2,1)} %param.30) | copy-start | bytes 98308
  3.6 16.6 %collective-permute-start = (f32[2,3,512]{2,1,0:T(4,128)S(1)}, f32[2,3,512]{2,1,0:T(4,128)S(1)}, u32[]{:S(2)}, u32[]{:S(2)}) collective-permute-start(f32[2,3,512]{2,1,0:T(4,128)S(1)} %get-tuple-element.396), channel_id=1, source_target_pairs={{0,1},{1,2},{2,3},{3,4},{4,5},{5,6},{6,7},{7,8},{8,9},{9,10},{10,1... | collective-permute-start | bytes 36872 | tf_op jit(solution)/shard_map/ppermute | solution.py:20
  3.7 16.6 %collective-permute-start.1 = (f32[2,3,512]{2,1,0:T(4,128)S(1)}, f32[2,3,512]{2,1,0:T(4,128)S(1)}, u32[]{:S(2)}, u32[]{:S(2)}) collective-permute-start(f32[2,3,512]{2,1,0:T(4,128)S(1)} %get-tuple-element.397), channel_id=1, source_target_pairs={{1,0},{2,1},{3,2},{4,3},{5,4},{6,5},{7,6},{8,7},{9,8},{10,9},{11,1... | collective-permute-start | bytes 36872 | tf_op jit(solution)/shard_map/ppermute | solution.py:22
  11.6 8.8 %collective-permute-start.2 = (bf16[512,128]{1,0:T(8,128)(2,1)S(1)}, bf16[512,128]{1,0:T(8,128)(2,1)S(1)}, u32[]{:S(2)}, u32[]{:S(2)}) collective-permute-start(bf16[512,128]{1,0:T(8,128)(2,1)S(1)} %get-tuple-element.390), channel_id=1, source_target_pairs={{0,1},{1,2},{2,3},{3,4},{4,5},{5,6},{6,7},{7,8},{8,9},{9,10},{10,1... | collective-permute-start | bytes 393224 | tf_op jit(solution)/shard_map/ppermute | solution.py:20
  11.7 8.7 %collective-permute-start.3 = (bf16[512,128]{1,0:T(8,128)(2,1)S(1)}, bf16[512,128]{1,0:T(8,128)(2,1)S(1)}, u32[]{:S(2)}, u32[]{:S(2)}) collective-permute-start(bf16[512,128]{1,0:T(8,128)(2,1)S(1)} %get-tuple-element.391), channel_id=1, source_target_pairs={{1,0},{2,1},{3,2},{4,3},{5,4},{6,5},{7,6},{8,7},{9,8},{10,9},{11,1... | collective-permute-start | bytes 393224 | tf_op jit(solution)/shard_map/ppermute | solution.py:22
  20.5 126.6 %copy-start.23 = (s32[1024]{0:T(1024)S(1)}, s32[1024]{0:T(1024)}, u32[]{:S(2)}) copy-start(s32[1024]{0:T(1024)} %param.24) | copy-start | bytes 12292
  20.8 30.3 %copy-start.2 = (bf16[2,8,1024,128]{3,2,1,0:T(8,128)(2,1)S(1)}, bf16[2,8,1024,128]{3,2,1,0:T(8,128)(2,1)}, u32[]{:S(2)}) copy-start(bf16[2,8,1024,128]{3,2,1,0:T(8,128)(2,1)} %get-tuple-element.585) | copy-start | bytes 12582916 | tf_op jit(solution)/shard_map/while
  83.9 30.3 %copy-start.2 = (bf16[2,8,1024,128]{3,2,1,0:T(8,128)(2,1)S(1)}, bf16[2,8,1024,128]{3,2,1,0:T(8,128)(2,1)}, u32[]{:S(2)}) copy-start(bf16[2,8,1024,128]{3,2,1,0:T(8,128)(2,1)} %get-tuple-element.585) | copy-start | bytes 12582916 | tf_op jit(solution)/shard_map/while
  148.2 9.2 %collective-permute-start.4 = (bf16[2,512,128]{1,2,0:T(8,128)(2,1)S(1)}, bf16[2,512,128]{1,2,0:T(8,128)(2,1)S(1)}, u32[]{:S(2)}, u32[]{:S(2)}) collective-permute-start(bf16[2,512,128]{1,2,0:T(8,128)(2,1)S(1)} %get-tuple-element.388), channel_id=1, source_target_pairs={{0,1},{1,2},{2,3},{3,4},{4,5},{5,6},{6,7},{7,8},{8,9},{9,10},{10,1... | collective-permute-start | bytes 786440 | tf_op jit(solution)/shard_map/ppermute | solution.py:20
  148.2 9.3 %collective-permute-start.5 = (bf16[2,512,128]{1,2,0:T(8,128)(2,1)S(1)}, bf16[2,512,128]{1,2,0:T(8,128)(2,1)S(1)}, u32[]{:S(2)}, u32[]{:S(2)}) collective-permute-start(bf16[2,512,128]{1,2,0:T(8,128)(2,1)S(1)} %get-tuple-element.389), channel_id=1, source_target_pairs={{1,0},{2,1},{3,2},{4,3},{5,4},{6,5},{7,6},{8,7},{9,8},{10,9},{11,1... | collective-permute-start | bytes 786440 | tf_op jit(solution)/shard_map/ppermute | solution.py:22
  157.8 84.7 %copy-start.11 = (f32[2,3,1024]{2,0,1:T(2,128)S(1)}, f32[2,3,1024]{2,0,1:T(2,128)}, u32[]{:S(2)}) copy-start(f32[2,3,1024]{2,0,1:T(2,128)} %param.20) | copy-start | bytes 73732
  157.8 84.7 %copy-start.20 = (f32[2,3,1024]{2,0,1:T(2,128)S(1)}, f32[2,3,1024]{2,0,1:T(2,128)}, u32[]{:S(2)}) copy-start(f32[2,3,1024]{2,0,1:T(2,128)} %param.21) | copy-start | bytes 73732
  157.8 84.7 %copy-start.22 = (f32[1024]{0:T(1024)S(1)}, f32[1024]{0:T(1024)}, u32[]{:S(2)}) copy-start(f32[1024]{0:T(1024)} %param.23) | copy-start | bytes 12292
  235.9 6.6 %collective-permute-start.6 = (f32[2,3,512]{2,1,0:T(4,128)S(1)}, f32[2,3,512]{2,1,0:T(4,128)S(1)}, u32[]{:S(2)}, u32[]{:S(2)}) collective-permute-start(f32[2,3,512]{2,1,0:T(4,128)S(1)} %get-tuple-element.394), channel_id=1, source_target_pairs={{0,1},{1,2},{2,3},{3,4},{4,5},{5,6},{6,7},{7,8},{8,9},{9,10},{10,1... | collective-permute-start | bytes 36872 | tf_op jit(solution)/shard_map/ppermute | solution.py:20
  236.0 6.5 %collective-permute-start.7 = (f32[2,3,512]{2,1,0:T(4,128)S(1)}, f32[2,3,512]{2,1,0:T(4,128)S(1)}, u32[]{:S(2)}, u32[]{:S(2)}) collective-permute-start(f32[2,3,512]{2,1,0:T(4,128)S(1)} %get-tuple-element.395), channel_id=1, source_target_pairs={{1,0},{2,1},{3,2},{4,3},{5,4},{6,5},{7,6},{8,7},{9,8},{10,9},{11,1... | collective-permute-start | bytes 36872 | tf_op jit(solution)/shard_map/ppermute | solution.py:22
  (10 other events, 88.0 us)
where the time goes:
time: 259 us
  matrix products  188 us (73%)
  other arithmetic  25.3 us (10%)
  starting transfers between devices  21.5 us (8%)
  blocking collectives  12.6 us (5%)
  local copies, waits for them, and re-layouts  4.88 us (2%)
  waiting for transfers between devices  4.75 us (2%)
    dot_general x2, matrix products, edge_geometry(): jnp.einsum('xe,sae->xsa', ext_pos, nbr_hot.astype(jnp.float32), precision...  60.5 us
    dot_general x2, matrix products, second_pass(): jnp.einsum('sae,ec->sac', nbr_hot, ext_feat, preferred_element_type=jnp.f...  35.1 us
    dot_general x2, matrix products, second_pass(): jnp.einsum('xsa,sae->xe', pair_force, nbr_hot.astype(jnp.float32), precis...  33.7 us
    dot_general x2, matrix products, first_pass(): jnp.einsum('sae,ec->sac', nbr_hot, species_ext, preferred_element_type=jn...  24.3 us
    dynamic_update_slice x2, other arithmetic, on_device(): lax.map(first_pass, (positions, pos_ext, neighbours, live_float))  22.6 us
    ppermute x4, starting transfers between devices, with_halo(): lax.ppermute(head, axis, [((i + 1) % count, i) for i in range(count)])  21.2 us
    dot_general x2, matrix products, edge_geometry(): jnp.einsum('sak,kc->sac', basis_vals, w_rad, precision=lax.Precision.HIGH...  16.5 us
    all_gather x1, blocking collectives, on_device(): everything = lax.all_gather(walker_state, 'walker', axis=0, tiled=True)  12.6 us
  transfers between devices with their start and end apart: 8, of which 2 were waited for; matrix products, arithmetic and copies ran while one was open for 2% of the time, Pallas kernels for 0%

commit v1 on v0

v1 whole, which is shorter than its diff:
```python
import functools
import math

import jax
import jax.numpy as jnp
from jax import lax
from jax.experimental import pallas as pl
from jax.experimental.pallas import tpu as pltpu
from jax.sharding import PartitionSpec as P

OFFSET = 2.0
CUTOFF = 5.0
STEP = 0.2
LANES = 128
MESH = pl.DeviceIdType.MESH
F32 = jnp.float32
BF16 = jnp.bfloat16


def lane_iota(shape):
    return lax.broadcasted_iota(jnp.int32, shape, len(shape) - 1)


def row_iota(shape):
    return lax.broadcasted_iota(jnp.int32, shape, 0)


def one_hot(column, width):
    rows = column.shape[0]
    wide = jnp.broadcast_to(column, (rows, LANES))
    lanes = lane_iota((rows, LANES))
    return jnp.concatenate(
        [(wide == lanes + j * LANES).astype(F32).astype(BF16) for j in range(width // LANES)], axis=1
    )


def silu(x):
    half = 0.5 * x
    return half + half * jnp.tanh(half)


def split(x):
    head = x.astype(BF16).astype(F32)
    return head, x - head


def dot(a, b):
    return jnp.dot(a, b, preferred_element_type=F32)


def lane_lookup(rows, hi, lo):
    found = jnp.zeros(lo.shape, F32)
    for r, row in enumerate(rows):
        picked = jnp.take_along_axis(
            jnp.broadcast_to(row, lo.shape), lo, axis=1, mode="promise_in_bounds"
        )
        found = jnp.where(hi == r, picked, found)
    return found


def kernel(
    pos, vel, spc, mas, send, nbr, liv, wrad, w1, w2, wup, wout, wts, bns, csr, csr_s,
    opos, ovel, onw,
    send_pos, halo_pos, send_spc, halo_spc, feat, send_feat, halo_feat, filt2, oh, send_oh,
    send_lo, gath, disp, wbig, sumw, wcat, acc, force, send_frc, recv_frc, every, prod,
    send_sem, recv_sem,
):
    n_walk, n_dom = lax.axis_size("walker"), lax.axis_size("domain")
    me_w, me_d = lax.axis_index("walker"), lax.axis_index("domain")
    left = lax.rem(me_d + n_dom - 1, n_dom)
    right = lax.rem(me_d + 1, n_dom)
    walkers, atoms = pos.shape[0], pos.shape[2]
    halo = send.shape[1] // 2
    groups = atoms // LANES
    slots = nbr.shape[1]
    tile_edges = slots * LANES
    peers = [(me_w, left), (me_w, right)]
    peers += [(lax.rem(me_w + o, n_walk), me_d) for o in range(1, n_walk)]

    barrier = pltpu.get_barrier_semaphore()
    for peer in peers:
        pl.semaphore_signal(barrier, inc=1, device_id=peer, device_id_type=MESH)

    def remote(src, dst, sem, peer):
        return pltpu.make_async_remote_copy(
            src_ref=src,
            dst_ref=dst,
            send_sem=send_sem.at[sem],
            recv_sem=recv_sem.at[sem],
            device_id=peer,
            device_id_type=MESH,
        )

    def both_ways(src, dst, sem):
        copies = [
            remote(src.at[0], dst.at[1], sem, peers[0]),
            remote(src.at[1], dst.at[0], sem + 1, peers[1]),
        ]
        for copy in copies:
            copy.start()
        return copies

    rows_out = jnp.concatenate(
        [send[:, g * LANES : (g + 1) * LANES] for g in range(groups)], axis=0
    )
    out_hi, out_lo = rows_out >> 7, rows_out & (LANES - 1)
    per_side = groups // 2
    for w in range(walkers):
        for c in range(3):
            table = [pos[w, c : c + 1, r * LANES : (r + 1) * LANES] for r in range(groups)]
            sent = lane_lookup(table, out_hi, out_lo)
            row = w * 3 + c
            for g in range(groups):
                q = g % per_side
                send_pos[g // per_side, row : row + 1, q * LANES : (q + 1) * LANES] = sent[g : g + 1]
    columns_out = jnp.transpose(rows_out)
    lo_out = jnp.transpose(out_lo)
    for g in range(groups):
        block = slice(g * LANES, (g + 1) * LANES)
        send_oh[block, :] = one_hot(columns_out[:, g : g + 1], atoms)
        send_lo[block, :] = one_hot(lo_out[:, g : g + 1], LANES)
    pl.semaphore_wait(barrier, len(peers))
    moves = both_ways(send_pos, halo_pos, 0)
    sent = dot(send_oh[...], spc[...]).astype(BF16)
    send_spc[0] = sent[:halo]
    send_spc[1] = sent[halo:]
    moves += both_ways(send_spc, halo_spc, 2)

    def weights_by_slot():
        heads, tails = split(wrad[...])
        sub = row_iota((slots, LANES))
        for s in range(slots):
            blocks = []
            for piece in (heads, tails):
                for _ in range(2):
                    for k in range(piece.shape[0]):
                        line = jnp.broadcast_to(piece[k : k + 1, :], (slots, LANES))
                        blocks.append(jnp.where(sub == s, line, 0.0))
            wbig[:, s * LANES : (s + 1) * LANES] = jnp.concatenate(blocks, axis=0).astype(BF16)

    weights_by_slot()
    for s in range(slots):
        sumw[s * 2 * LANES : (s + 1) * 2 * LANES, :] = (
            (lane_iota((2 * LANES, LANES)) == s).astype(F32).astype(BF16)
        )
    wcat[:, :LANES] = w1[...]
    wcat[:, LANES:] = w2[...]

    count = wts.shape[1]
    square = (count, count)
    eye = (lane_iota(square) == row_iota(square)).astype(F32)

    def to_column(row):
        return jnp.sum(eye * row, axis=1, keepdims=True)

    def to_row(column):
        return jnp.sum(eye * column, axis=0, keepdims=True)

    w_row, b_row = wts[...], bns[...].astype(F32)
    chosen = (to_column(csr[...].astype(F32)) == lane_iota(square).astype(F32)).astype(F32)
    src_w = jnp.sum(chosen * w_row, axis=1, keepdims=True)
    src_b = jnp.sum(chosen * b_row, axis=1, keepdims=True)
    mass = jnp.sum((src_b == b_row).astype(F32) * w_row, axis=1, keepdims=True)
    share = jnp.sum((src_b == to_row(src_b)).astype(F32) * to_row(src_w), axis=1, keepdims=True)
    onw[...] = to_row(mass * src_w / share)

    for copy in moves:
        copy.wait()

    def edge_ids(w, at):
        ids = nbr[w, :, at]
        key = (ids >> 10) * halo + (ids & (halo - 1))
        key = jnp.where(liv[w, :, at] != 0, key, -1)
        return ids, key, (ids >> 9) & 1

    def gather_rows(key, second, own, near):
        key_t = jnp.transpose(key)
        second_t = jnp.transpose(second)
        for s in range(slots):
            oh[s * LANES : (s + 1) * LANES, :] = one_hot(key_t[:, s : s + 1], 2 * halo)
        table = jnp.concatenate(
            [
                jnp.concatenate([own[:halo], own[halo:]], axis=1),
                jnp.concatenate([near[0], near[1]], axis=1),
            ],
            axis=0,
        )
        both = dot(oh[...], table)
        for s in range(slots):
            block = slice(s * LANES, (s + 1) * LANES)
            take = jnp.broadcast_to(second_t[:, s : s + 1], (LANES, LANES)) != 0
            gath[block, :] = jnp.where(take, both[block, LANES:], both[block, :LANES])

    def geometry(w, at, ids):
        hi, lo = ids >> 7, ids & (LANES - 1)
        square_sum = None
        for c in range(3):
            table = [pos[w, c : c + 1, r * LANES : (r + 1) * LANES] for r in range(groups)]
            for side in range(2):
                shift = 0.0 if c else (OFFSET if side else -OFFSET)
                for q in range(per_side):
                    row = w * 3 + c
                    table.append(
                        halo_pos[side, row : row + 1, q * LANES : (q + 1) * LANES] + shift
                    )
            delta = lane_lookup(table, hi, lo) - pos[w, c : c + 1, at]
            disp[w, c, :, at] = delta
            square_sum = delta * delta if c == 0 else square_sum + delta * delta
        scaled = jnp.sqrt(square_sum) / CUTOFF
        envelope = jnp.square(jnp.maximum(0.0, 1.0 - scaled * scaled))
        first = jnp.cos(jnp.minimum(scaled, 1.0) * math.pi)
        waves = [first, 2.0 * first * first - 1.0]
        while len(waves) < wrad.shape[0]:
            waves.append(2.0 * first * waves[-1] - waves[-2])
        pieces = [split(wave * envelope) for wave in waves]
        stacked = jnp.concatenate([p[0] for p in pieces] + [p[1] for p in pieces], axis=0)
        turned = jnp.transpose(stacked).astype(BF16)
        return jnp.concatenate([turned, turned], axis=1)

    def first_pass(w, t):
        at = pl.ds(pl.multiple_of(t * LANES, LANES), LANES)
        ids, key, second = edge_ids(w, at)
        basis = geometry(w, at, ids)
        gather_rows(key, second, spc[...], halo_spc)
        total = jnp.zeros((LANES, LANES), F32)
        for s in range(0, slots, 2):
            hidden = dot(basis, wbig[:, s * LANES : (s + 2) * LANES])
            radial = silu(hidden).astype(BF16)
            for i in range(2):
                block = slice((s + i) * LANES, (s + i + 1) * LANES)
                filters = dot(radial[:, i * LANES : (i + 1) * LANES], wcat[...])
                filt2[w, t, block, :] = filters[:, LANES:]
                total = total + filters[:, :LANES] * gath[block, :]
        updated = dot(total.astype(BF16), wup[...])
        feat[w, at, :] = (spc[at, :].astype(F32) + silu(updated)).astype(BF16)

    def second_pass(w, t):
        at = pl.ds(pl.multiple_of(t * LANES, LANES), LANES)
        ids, key, second = edge_ids(w, at)
        gather_rows(key, second, feat[w], halo_feat[w])
        own = feat[w, at, :].astype(F32) * wout[...]
        for s in range(slots):
            block = slice(s * LANES, (s + 1) * LANES)
            head, tail = split(filt2[w, t, block, :] * own * gath[block, :])
            prod[:, 2 * s * LANES : (2 * s + 1) * LANES] = head.astype(BF16)
            prod[:, (2 * s + 1) * LANES : (2 * s + 2) * LANES] = tail.astype(BF16)
        coupling = jnp.transpose(dot(prod[...], sumw[...]))[:slots]
        hi, lo = ids >> 7, ids & (LANES - 1)
        pieces = []
        for c in range(3):
            pair = coupling * disp[w, c, :, at]
            force[w, c, pl.ds(t, 1), :] = jnp.sum(pair, axis=0, keepdims=True)
            pieces.append(split(pair))
        acc[...] += spread(pieces, hi, lo, 2 * groups)

    def spread_left(pieces, hi, high_count):
        sub = row_iota((high_count, LANES))
        out = []
        for s in range(hi.shape[0]):
            here = jnp.broadcast_to(hi[s : s + 1], (high_count, LANES)) == sub
            rows = [
                jnp.where(here, jnp.broadcast_to(x[p][s : s + 1], (high_count, LANES)), 0.0)
                for p in range(2)
                for x in pieces
            ]
            out.append(jnp.concatenate(rows, axis=0).astype(BF16))
        return jnp.concatenate(out, axis=1)

    def spread(pieces, hi, lo, high_count):
        lo_t = jnp.transpose(lo)
        low = jnp.concatenate([one_hot(lo_t[:, s : s + 1], LANES) for s in range(slots)], axis=0)
        return dot(spread_left(pieces, hi, high_count), low)

    def loop(body, w):
        def step(t, carry):
            body(w, t)
            return carry

        lax.fori_loop(0, groups, step, 0)

    feat_moves = []
    for w in range(walkers):
        loop(first_pass, w)
        sent = dot(send_oh[...], feat[w]).astype(BF16)
        send_feat[w, 0] = sent[:halo]
        send_feat[w, 1] = sent[halo:]
        feat_moves.append(both_ways(send_feat.at[w], halo_feat.at[w], 4 + 2 * w))

    force_moves = []
    high = 2 * groups
    for w in range(walkers):
        for copy in feat_moves[w]:
            copy.wait()
        acc[...] = jnp.zeros_like(acc)
        loop(second_pass, w)
        reaction = acc[: 3 * high] + acc[3 * high :]
        for c in range(3):
            force[w, c] = force[w, c] - reaction[c * high : c * high + groups]
            for side in range(2):
                start = c * high + groups + side * per_side
                send_frc[w, side, c * per_side : (c + 1) * per_side, :] = -reaction[
                    start : start + per_side
                ]
        base = 4 + 2 * walkers + 2 * w
        force_moves.append(both_ways(send_frc.at[w], recv_frc.at[w], base))

    state_moves = []
    for w in range(walkers):
        for copy in force_moves[w]:
            copy.wait()
        pieces = []
        for c in range(3):
            rows = slice(c * per_side, (c + 1) * per_side)
            pieces.append(
                split(jnp.concatenate([recv_frc[w, 0, rows, :], recv_frc[w, 1, rows, :]], axis=0))
            )
        back = dot(spread_left(pieces, out_hi, groups), send_lo[...])
        for c in range(3):
            total = force[w, c] + (
                back[c * groups : (c + 1) * groups]
                + back[(3 + c) * groups : (4 + c) * groups]
            )
            flat = jnp.concatenate([total[g : g + 1] for g in range(groups)], axis=1)
            stepped = vel[w, c : c + 1, :] + STEP * flat / mas[...]
            every[w, c : c + 1, :] = pos[w, c : c + 1, :] + STEP * stepped
            every[w, 3 + c : 4 + c, :] = stepped
        for o in range(1, n_walk):
            base = 4 + 4 * walkers + w * (n_walk - 1) + o - 1
            copy = remote(every.at[w], every.at[o * walkers + w], base, peers[1 + o])
            copy.start()
            state_moves.append(copy)
    for copy in state_moves:
        copy.wait()
    for k in range(walkers):
        source = csr_s[me_w * walkers + k]
        behind = lax.rem(me_w - lax.div(source, walkers) + n_walk, n_walk)
        picked = every[behind * walkers + lax.rem(source, walkers)]
        opos[k] = picked[:3]
        ovel[k] = picked[3:6]


def on_device(
    positions,
    velocities,
    species,
    masses,
    send_rows,
    neighbours,
    live_edges,
    w_rad,
    w_first,
    w_second,
    w_update,
    w_out,
    weights,
    bins,
    copy_src,
):
    walkers, _, atoms = positions.shape
    channels = species.shape[1]
    halo = send_rows.shape[0] // 2
    groups = atoms // LANES
    slots = neighbours.shape[1]
    orders = w_rad.shape[0]
    n_walk = lax.axis_size("walker")
    edges = slots * LANES
    copies = 4 + 4 * walkers + walkers * (n_walk - 1)
    vmem = pl.BlockSpec(memory_space=pltpu.VMEM)
    smem = pl.BlockSpec(memory_space=pltpu.SMEM)
    halo_rows = (2, halo, channels)
    out_positions, out_velocities, new_weights = pl.pallas_call(
        kernel,
        out_shape=(
            jax.ShapeDtypeStruct(positions.shape, F32),
            jax.ShapeDtypeStruct(velocities.shape, F32),
            jax.ShapeDtypeStruct((1, weights.shape[0]), F32),
        ),
        in_specs=[vmem] * 15 + [smem],
        out_specs=(vmem, vmem, vmem),
        scratch_shapes=[
            pltpu.VMEM((2, 8, halo), F32),
            pltpu.VMEM((2, 8, halo), F32),
            pltpu.VMEM(halo_rows, BF16),
            pltpu.VMEM(halo_rows, BF16),
            pltpu.VMEM((walkers, atoms, channels), BF16),
            pltpu.VMEM((walkers, *halo_rows), BF16),
            pltpu.VMEM((walkers, *halo_rows), BF16),
            pltpu.VMEM((walkers, groups, edges, channels), F32),
            pltpu.VMEM((edges, 2 * halo), BF16),
            pltpu.VMEM((2 * halo, atoms), BF16),
            pltpu.VMEM((2 * halo, LANES), BF16),
            pltpu.VMEM((edges, channels), F32),
            pltpu.VMEM((walkers, 3, slots, atoms), F32),
            pltpu.VMEM((4 * orders * slots, slots * channels), BF16),
            pltpu.VMEM((slots * 2 * channels, LANES), BF16),
            pltpu.VMEM((channels, 2 * channels), BF16),
            pltpu.VMEM((12 * groups, LANES), F32),
            pltpu.VMEM((walkers, 3, groups, LANES), F32),
            pltpu.VMEM((walkers, 2, 16, LANES), F32),
            pltpu.VMEM((walkers, 2, 16, LANES), F32),
            pltpu.VMEM((n_walk * walkers, 8, atoms), F32),
            pltpu.VMEM((LANES, slots * 2 * channels), BF16),
            pltpu.SemaphoreType.DMA((copies,)),
            pltpu.SemaphoreType.DMA((copies,)),
        ],
        compiler_params=pltpu.CompilerParams(
            collective_id=0, has_side_effects=True, vmem_limit_bytes=48 * 2**20
        ),
    )(
        positions,
        velocities,
        species,
        masses[None],
        send_rows[None],
        neighbours,
        live_edges,
        w_rad,
        w_first,
        w_second,
        w_update,
        w_out[None],
        weights[None],
        bins[None],
        copy_src[None],
        copy_src,
    )
    return out_positions, out_velocities, new_weights[0]


def solution(mesh):
    in_specs = (
        P("walker", None, "domain"),
        P("walker", None, "domain"),
        P("domain", None),
        P("domain"),
        P("domain"),
        P("walker", None, "domain"),
        P("walker", None, "domain"),
        P(),
        P(),
        P(),
        P(),
        P(),
        P(),
        P(),
        P(),
    )
    out_specs = (P("walker", None, "domain"), P("walker", None, "domain"), P())
    return jax.shard_map(
        on_device, mesh=mesh, in_specs=in_specs, out_specs=out_specs, check_vma=False
    )
```

time: 259 us -> 91.2 us (0.35)
  matrix products: 188 us -> 0 us
  Pallas kernels: 0 us -> 83.3 us
  other arithmetic: 25.3 us -> 0 us
  starting transfers between devices: 21.5 us -> 0 us
  blocking collectives: 12.6 us -> 0 us
  waiting for transfers between devices: 4.75 us -> 0 us
    dot_general x20 -> x0, matrix products: 188 us -> none  [the longest x2 60.5 us: edge_geometry(): jnp.einsum('xe,sae->xsa', ext_pos, nbr_hot.astype(jnp.float32), precision...]
    pallas_call x0 -> x1, Pallas kernels: none -> 83.3 us  [on_device(): pl.pallas_call(kernel, out_shape=(jax.ShapeDtypeStruct(positions.shape, F...]
    dynamic_update_slice x4 -> x0, other arithmetic: 22.6 us -> none  [the longest x2 22.6 us: on_device(): lax.map(first_pass, (positions, pos_ext, neighbours, live_float))]
    ppermute x8 -> x0, starting transfers between devices: 21.5 us -> none  [the longest x4 21.2 us: with_halo(): lax.ppermute(head, axis, [((i + 1) % count, i) for i in range(count)])]
    all_gather x1 -> x0, blocking collectives: 12.6 us -> none  [on_device(): everything = lax.all_gather(walker_state, 'walker', axis=0, tiled=True)]
    unnamed x47 -> x31, local copies, waits for them, and re-layouts: 1.39 us -> 6.69 us
    ppermute x8 -> x0, waiting for transfers between devices: 4.75 us -> none  [the longest x4 4.72 us: with_halo(): lax.ppermute(tail, axis, [(i, (i + 1) % count) for i in range(count)])]
  transfers between devices with their start and end apart: 8 -> 0, of which waited for: 2 -> 0; matrix products, arithmetic and copies ran while one was open for 2% -> 0% of each run, Pallas kernels for 0% -> 0%
where the time goes in v1:
time: 91.2 us; the launch traced here: 90.8 us
  Pallas kernels  83.3 us (91%)
  local copies, waits for them, and re-layouts  6.69 us (7%)
    pallas_call x1, Pallas kernels, on_device(): pl.pallas_call(kernel, out_shape=(jax.ShapeDtypeStruct(positions.shape, F...  83.3 us
    unnamed x31, local copies, waits for them, and re-layouts  6.69 us

profile of v1, /device:TPU:0, one launch (start us, length us, event | category | flops | bytes accessed | tf_op | source)
XLA Modules:
  0.0 90.8 jit_solution(4675784463700658179)
XLA Ops:
  0.6 0.0 copy-start.1
  0.6 0.8 copy.18.pos
  1.4 0.0 copy-start.3
  1.4 0.0 copy-start.6
  1.4 0.0 copy-start.7
  1.5 0.0 copy-start.8
  1.5 0.0 copy-start.9
  1.5 0.0 copy-start.10
  1.5 0.0 copy-start.11
  1.5 0.0 copy-start.12
  1.5 0.8 copy.19.vel
  2.3 0.0 copy-done.1
  2.3 0.0 copy-done.3
  2.3 0.0 copy-done.6
  2.3 0.0 copy-done.7
  2.4 0.0 copy-start
  2.4 0.9 %copy-done = bf16[1024,128]{1,0:T(8,128)(2,1)S(1)} copy-done((bf16[1024,128]{1,0:T(8,128)(2,1)S(1)}, bf16[1024,128]{1,0:T(8,128)(2,1)}, u32[]{:S(2)}) %copy-start) | copy-done | bytes 262168
  3.4 0.8 copy-done.2
  4.2 0.8 copy-done.4
  5.0 0.8 copy-done.5
  5.7 83.3 %shard_map.166 = (f32[2,3,1024]{2,1,0:T(4,128)S(1)}, f32[2,3,1024]{2,1,0:T(4,128)S(1)}, f32[1,8]{1,0:T(1,128)S(1)}) custom-call(f32[2,3,1024]{2,1,0:T(4,128)S(1)} %copy.18.pos, f32[2,3,1024]{2,1,0:T(4,128)S(1)} %copy.19.vel, bf16[1024,128]{1,0:T(8,128)(2,1)S(1)} %copy-done, f32[1,1024]{1,0:T(1,128)S(1)} %bitcast.7, s32[1,1024]{1,0:T(1,128)S(1)} %bitcast.8, ...), custom_call_target="tpu_custom_call" | custom-call | tf_op jit(solution)/shard_map/pallas_call | solution.py:371
  89.0 0.6 copy.20
  89.6 0.6 copy.21
  90.2 0.5 copy.23
  (8 shorter events, 0.0 us)
Async XLA Ops:
  0.6 1.7 %copy-start.1 = (s32[2,8,1024]{2,1,0:T(8,128)S(1)}, s32[2,8,1024]{2,1,0:T(8,128)}, u32[]{:S(2)}) copy-start(s32[2,8,1024]{2,1,0:T(8,128)} %nbr.1) | copy-start | bytes 196612
  1.4 0.9 copy-start.3
  1.4 0.9 copy-start.6
  1.4 0.9 copy-start.7
  1.5 0.9 copy-start.8
  1.5 0.9 copy-start.9
  1.5 0.9 copy-start.10
  1.5 0.9 copy-start.11
  1.5 0.9 copy-start.12
  2.4 1.0 %copy-start = (bf16[1024,128]{1,0:T(8,128)(2,1)S(1)}, bf16[1024,128]{1,0:T(8,128)(2,1)}, u32[]{:S(2)}) copy-start(bf16[1024,128]{1,0:T(8,128)(2,1)} %spc.1) | copy-start | bytes 786436
  3.4 0.8 copy-start.2
  4.2 0.8 copy-start.4
  5.0 0.8 copy-start.5

commit v2 on v1

--- a/solution.py
+++ b/solution.py
@@ -27,10 +27,15 @@
 
 def one_hot(column, width):
     rows = column.shape[0]
-    wide = jnp.broadcast_to(column, (rows, LANES))
+    wide = jnp.broadcast_to(column, (rows, LANES)).astype(jnp.int16)
     lanes = lane_iota((rows, LANES))
+    one, zero = jnp.ones((rows, LANES), BF16), jnp.zeros((rows, LANES), BF16)
     return jnp.concatenate(
-        [(wide == lanes + j * LANES).astype(F32).astype(BF16) for j in range(width // LANES)], axis=1
+        [
+            jnp.where(wide == (lanes + j * LANES).astype(jnp.int16), one, zero)
+            for j in range(width // LANES)
+        ],
+        axis=1,
     )
 
 
@@ -59,17 +64,19 @@
 
 
 def kernel(
-    pos, vel, spc, mas, send, nbr, liv, wrad, w1, w2, wup, wout, wts, bns, csr, csr_s,
+    pos_h, vel_h, spc_h, mas_h, send_h, nbr_h, liv_h, wrad_h, w1_h, w2_h, wup_h, wout_h,
+    wts, bns, csr, csr_s,
     opos, ovel, onw,
+    pos, vel, spc, mas, send, nbr, liv, wrad, w1, w2, wup, wout,
     send_pos, halo_pos, send_spc, halo_spc, feat, send_feat, halo_feat, filt2, oh, send_oh,
-    send_lo, gath, disp, wbig, sumw, wcat, acc, force, send_frc, recv_frc, every, prod,
-    send_sem, recv_sem,
+    send_lo, low, gath, disp, wbig, sumw, wcat, acc, force, send_frc, recv_frc, every, prod,
+    load_sem, send_sem, recv_sem,
 ):
     n_walk, n_dom = lax.axis_size("walker"), lax.axis_size("domain")
     me_w, me_d = lax.axis_index("walker"), lax.axis_index("domain")
     left = lax.rem(me_d + n_dom - 1, n_dom)
     right = lax.rem(me_d + 1, n_dom)
-    walkers, atoms = pos.shape[0], pos.shape[2]
+    walkers, atoms = pos.shape[1], pos.shape[2]
     halo = send.shape[1] // 2
     groups = atoms // LANES
     slots = nbr.shape[1]
@@ -80,6 +87,26 @@
     barrier = pltpu.get_barrier_semaphore()
     for peer in peers:
         pl.semaphore_signal(barrier, inc=1, device_id=peer, device_id_type=MESH)
+
+    loads = {}
+    for i, (name, src, dst) in enumerate(
+        [
+            ("send", send_h, send),
+            ("pos", pos_h, pos),
+            ("spc", spc_h, spc),
+            ("nbr", nbr_h, nbr),
+            ("liv", liv_h, liv),
+            ("wrad", wrad_h, wrad),
+            ("w1", w1_h, w1),
+            ("w2", w2_h, w2),
+            ("wup", wup_h, wup),
+            ("wout", wout_h, wout),
+            ("vel", vel_h, vel),
+            ("mas", mas_h, mas),
+        ]
+    ):
+        loads[name] = pltpu.make_async_copy(src, dst, load_sem.at[i])
+        loads[name].start()
 
     def remote(src, dst, sem, peer):
         return pltpu.make_async_remote_copy(
@@ -100,6 +127,8 @@
             copy.start()
         return copies
 
+    loads["send"].wait()
+    loads["pos"].wait()
     rows_out = jnp.concatenate(
         [send[:, g * LANES : (g + 1) * LANES] for g in range(groups)], axis=0
     )
@@ -107,7 +136,7 @@
     per_side = groups // 2
     for w in range(walkers):
         for c in range(3):
-            table = [pos[w, c : c + 1, r * LANES : (r + 1) * LANES] for r in range(groups)]
+            table = [pos[c, w : w + 1, r * LANES : (r + 1) * LANES] for r in range(groups)]
             sent = lane_lookup(table, out_hi, out_lo)
             row = w * 3 + c
             for g in range(groups):
@@ -119,12 +148,16 @@
         block = slice(g * LANES, (g + 1) * LANES)
         send_oh[block, :] = one_hot(columns_out[:, g : g + 1], atoms)
         send_lo[block, :] = one_hot(lo_out[:, g : g + 1], LANES)
+    loads["spc"].wait()
     pl.semaphore_wait(barrier, len(peers))
     moves = both_ways(send_pos, halo_pos, 0)
     sent = dot(send_oh[...], spc[...]).astype(BF16)
     send_spc[0] = sent[:halo]
     send_spc[1] = sent[halo:]
     moves += both_ways(send_spc, halo_spc, 2)
+
+    for name in ("nbr", "liv", "wrad", "w1", "w2", "wup", "wout", "vel", "mas"):
+        loads[name].wait()
 
     def weights_by_slot():
         heads, tails = split(wrad[...])
@@ -164,20 +197,19 @@
     share = jnp.sum((src_b == to_row(src_b)).astype(F32) * to_row(src_w), axis=1, keepdims=True)
     onw[...] = to_row(mass * src_w / share)
 
-    for copy in moves:
-        copy.wait()
-
-    def edge_ids(w, at):
+    def build(w, t):
+        at = pl.ds(pl.multiple_of(t * LANES, LANES), LANES)
         ids = nbr[w, :, at]
         key = (ids >> 10) * halo + (ids & (halo - 1))
-        key = jnp.where(liv[w, :, at] != 0, key, -1)
-        return ids, key, (ids >> 9) & 1
-
-    def gather_rows(key, second, own, near):
-        key_t = jnp.transpose(key)
-        second_t = jnp.transpose(second)
+        key_t = jnp.transpose(jnp.where(liv[w, :, at] != 0, key, -1))
+        lo_t = jnp.transpose(ids & (LANES - 1))
         for s in range(slots):
-            oh[s * LANES : (s + 1) * LANES, :] = one_hot(key_t[:, s : s + 1], 2 * halo)
+            block = slice(s * LANES, (s + 1) * LANES)
+            oh[w, t, block, :] = one_hot(key_t[:, s : s + 1], 2 * halo)
+            low[w, t, block, :] = one_hot(lo_t[:, s : s + 1], LANES)
+
+    def gather_rows(w, t, ids, own, near):
+        second_t = jnp.transpose((ids >> 9) & 1)
         table = jnp.concatenate(
             [
                 jnp.concatenate([own[:halo], own[halo:]], axis=1),
@@ -185,7 +217,7 @@
             ],
             axis=0,
         )
-        both = dot(oh[...], table)
+        both = dot(oh[w, t], table)
         for s in range(slots):
             block = slice(s * LANES, (s + 1) * LANES)
             take = jnp.broadcast_to(second_t[:, s : s + 1], (LANES, LANES)) != 0
@@ -195,7 +227,7 @@
         hi, lo = ids >> 7, ids & (LANES - 1)
         square_sum = None
         for c in range(3):
-            table = [pos[w, c : c + 1, r * LANES : (r + 1) * LANES] for r in range(groups)]
+            table = [pos[c, w : w + 1, r * LANES : (r + 1) * LANES] for r in range(groups)]
             for side in range(2):
                 shift = 0.0 if c else (OFFSET if side else -OFFSET)
                 for q in range(per_side):
@@ -203,7 +235,7 @@
                     table.append(
                         halo_pos[side, row : row + 1, q * LANES : (q + 1) * LANES] + shift
                     )
-            delta = lane_lookup(table, hi, lo) - pos[w, c : c + 1, at]
+            delta = lane_lookup(table, hi, lo) - pos[c, w : w + 1, at]
             disp[w, c, :, at] = delta
             square_sum = delta * delta if c == 0 else square_sum + delta * delta
         scaled = jnp.sqrt(square_sum) / CUTOFF
@@ -219,9 +251,9 @@
 
     def first_pass(w, t):
         at = pl.ds(pl.multiple_of(t * LANES, LANES), LANES)
-        ids, key, second = edge_ids(w, at)
+        ids = nbr[w, :, at]
         basis = geometry(w, at, ids)
-        gather_rows(key, second, spc[...], halo_spc)
+        gather_rows(w, t, ids, spc[...], halo_spc)
         total = jnp.zeros((LANES, LANES), F32)
         for s in range(0, slots, 2):
             hidden = dot(basis, wbig[:, s * LANES : (s + 2) * LANES])
@@ -236,8 +268,8 @@
 
     def second_pass(w, t):
         at = pl.ds(pl.multiple_of(t * LANES, LANES), LANES)
-        ids, key, second = edge_ids(w, at)
-        gather_rows(key, second, feat[w], halo_feat[w])
+        ids = nbr[w, :, at]
+        gather_rows(w, t, ids, feat[w], halo_feat[w])
         own = feat[w, at, :].astype(F32) * wout[...]
         for s in range(slots):
             block = slice(s * LANES, (s + 1) * LANES)
@@ -245,13 +277,13 @@
             prod[:, 2 * s * LANES : (2 * s + 1) * LANES] = head.astype(BF16)
             prod[:, (2 * s + 1) * LANES : (2 * s + 2) * LANES] = tail.astype(BF16)
         coupling = jnp.transpose(dot(prod[...], sumw[...]))[:slots]
-        hi, lo = ids >> 7, ids & (LANES - 1)
+        hi = ids >> 7
         pieces = []
         for c in range(3):
             pair = coupling * disp[w, c, :, at]
             force[w, c, pl.ds(t, 1), :] = jnp.sum(pair, axis=0, keepdims=True)
             pieces.append(split(pair))
-        acc[...] += spread(pieces, hi, lo, 2 * groups)
+        acc[...] += dot(spread_left(pieces, hi, 2 * groups), low[w, t])
 
     def spread_left(pieces, hi, high_count):
         sub = row_iota((high_count, LANES))
@@ -266,11 +298,6 @@
             out.append(jnp.concatenate(rows, axis=0).astype(BF16))
         return jnp.concatenate(out, axis=1)
 
-    def spread(pieces, hi, lo, high_count):
-        lo_t = jnp.transpose(lo)
-        low = jnp.concatenate([one_hot(lo_t[:, s : s + 1], LANES) for s in range(slots)], axis=0)
-        return dot(spread_left(pieces, hi, high_count), low)
-
     def loop(body, w):
         def step(t, carry):
             body(w, t)
@@ -278,8 +305,13 @@
 
         lax.fori_loop(0, groups, step, 0)
 
+    loop(build, 0)
+    for copy in moves:
+        copy.wait()
     feat_moves = []
     for w in range(walkers):
+        if w:
+            loop(build, w)
         loop(first_pass, w)
         sent = dot(send_oh[...], feat[w]).astype(BF16)
         send_feat[w, 0] = sent[:halo]
@@ -321,8 +353,8 @@
                 + back[(3 + c) * groups : (4 + c) * groups]
             )
             flat = jnp.concatenate([total[g : g + 1] for g in range(groups)], axis=1)
-            stepped = vel[w, c : c + 1, :] + STEP * flat / mas[...]
-            every[w, c : c + 1, :] = pos[w, c : c + 1, :] + STEP * stepped
+            stepped = vel[c, w : w + 1, :] + STEP * flat / mas[...]
+            every[w, c : c + 1, :] = pos[c, w : w + 1, :] + STEP * stepped
             every[w, 3 + c : 4 + c, :] = stepped
         for o in range(1, n_walk):
             base = 4 + 4 * walkers + w * (n_walk - 1) + o - 1
@@ -335,8 +367,9 @@
         source = csr_s[me_w * walkers + k]
         behind = lax.rem(me_w - lax.div(source, walkers) + n_walk, n_walk)
         picked = every[behind * walkers + lax.rem(source, walkers)]
-        opos[k] = picked[:3]
-        ovel[k] = picked[3:6]
+        for c in range(3):
+            opos[c, k : k + 1, :] = picked[c : c + 1]
+            ovel[c, k : k + 1, :] = picked[3 + c : 4 + c]
 
 
 def on_device(
@@ -365,19 +398,33 @@
     n_walk = lax.axis_size("walker")
     edges = slots * LANES
     copies = 4 + 4 * walkers + walkers * (n_walk - 1)
+    by_component = (3, walkers, atoms)
+    hbm = pl.BlockSpec(memory_space=pltpu.HBM)
     vmem = pl.BlockSpec(memory_space=pltpu.VMEM)
     smem = pl.BlockSpec(memory_space=pltpu.SMEM)
     halo_rows = (2, halo, channels)
     out_positions, out_velocities, new_weights = pl.pallas_call(
         kernel,
         out_shape=(
-            jax.ShapeDtypeStruct(positions.shape, F32),
-            jax.ShapeDtypeStruct(velocities.shape, F32),
+            jax.ShapeDtypeStruct(by_component, F32),
+            jax.ShapeDtypeStruct(by_component, F32),
             jax.ShapeDtypeStruct((1, weights.shape[0]), F32),
         ),
-        in_specs=[vmem] * 15 + [smem],
+        in_specs=[hbm] * 12 + [vmem] * 3 + [smem],
         out_specs=(vmem, vmem, vmem),
         scratch_shapes=[
+            pltpu.VMEM(by_component, F32),
+            pltpu.VMEM(by_component, F32),
+            pltpu.VMEM(species.shape, BF16),
+            pltpu.VMEM((1, atoms), F32),
+            pltpu.VMEM((1, 2 * halo), jnp.int32),
+            pltpu.VMEM(neighbours.shape, jnp.int32),
+            pltpu.VMEM(live_edges.shape, jnp.int32),
+            pltpu.VMEM(w_rad.shape, F32),
+            pltpu.VMEM(w_first.shape, BF16),
+            pltpu.VMEM(w_second.shape, BF16),
+            pltpu.VMEM(w_update.shape, BF16),
+            pltpu.VMEM((1, channels), F32),
             pltpu.VMEM((2, 8, halo), F32),
             pltpu.VMEM((2, 8, halo), F32),
             pltpu.VMEM(halo_rows, BF16),
@@ -386,9 +433,10 @@
             pltpu.VMEM((walkers, *halo_rows), BF16),
             pltpu.VMEM((walkers, *halo_rows), BF16),
             pltpu.VMEM((walkers, groups, edges, channels), F32),
-            pltpu.VMEM((edges, 2 * halo), BF16),
+            pltpu.VMEM((walkers, groups, edges, 2 * halo), BF16),
             pltpu.VMEM((2 * halo, atoms), BF16),
             pltpu.VMEM((2 * halo, LANES), BF16),
+            pltpu.VMEM((walkers, groups, edges, LANES), BF16),
             pltpu.VMEM((edges, channels), F32),
             pltpu.VMEM((walkers, 3, slots, atoms), F32),
             pltpu.VMEM((4 * orders * slots, slots * channels), BF16),
@@ -400,15 +448,16 @@
             pltpu.VMEM((walkers, 2, 16, LANES), F32),
             pltpu.VMEM((n_walk * walkers, 8, atoms), F32),
             pltpu.VMEM((LANES, slots * 2 * channels), BF16),
+            pltpu.SemaphoreType.DMA((12,)),
             pltpu.SemaphoreType.DMA((copies,)),
             pltpu.SemaphoreType.DMA((copies,)),
         ],
         compiler_params=pltpu.CompilerParams(
-            collective_id=0, has_side_effects=True, vmem_limit_bytes=48 * 2**20
+            collective_id=0, has_side_effects=True, vmem_limit_bytes=58 * 2**20
         ),
     )(
-        positions,
-        velocities,
+        jnp.transpose(positions, (1, 0, 2)),
+        jnp.transpose(velocities, (1, 0, 2)),
         species,
         masses[None],
         send_rows[None],
@@ -424,7 +473,11 @@
         copy_src[None],
         copy_src,
     )
-    return out_positions, out_velocities, new_weights[0]
+    return (
+        jnp.transpose(out_positions, (1, 0, 2)),
+        jnp.transpose(out_velocities, (1, 0, 2)),
+        new_weights[0],
+    )
 
 
 def solution(mesh):

time: 91.2 us -> 77.3 us (0.85)
  Pallas kernels: 83.3 us -> 73.9 us
  local copies, waits for them, and re-layouts: 6.69 us -> 2.55 us
    pallas_call x1, Pallas kernels: 83.3 us -> 73.9 us  [on_device(): pl.pallas_call(kernel, out_shape=(jax.ShapeDtypeStruct(by_component, F32)...]
    unnamed x31 -> x7, local copies, waits for them, and re-layouts: 6.69 us -> 2.55 us
where the time goes in v2:
time: 77.3 us; the launch traced here: 77.1 us
  Pallas kernels  73.9 us (96%)
  local copies, waits for them, and re-layouts  2.55 us (3%)
    pallas_call x1, Pallas kernels, on_device(): pl.pallas_call(kernel, out_shape=(jax.ShapeDtypeStruct(by_component, F32)...  73.9 us
    unnamed x7, local copies, waits for them, and re-layouts  2.55 us

profile of v2, /device:TPU:0, one launch (start us, length us, event | category | flops | bytes accessed | tf_op | source)
XLA Modules:
  0.0 77.1 jit_solution(9094252931090966109)
XLA Ops:
  0.6 73.9 %shard_map.166 = (f32[3,2,1024]{2,1,0:T(2,128)}, f32[3,2,1024]{2,1,0:T(2,128)}, f32[1,8]{1,0:T(1,128)}) custom-call(f32[3,2,1024]{2,1,0:T(2,128)} %bitcast.11, f32[3,2,1024]{2,1,0:T(2,128)} %bitcast.12, bf16[1024,128]{1,0:T(8,128)(2,1)} %spc_h.1, f32[1,1024]{1,0:T(1,128)} %bitcast.15, s32[1,1024]{1,0:T(1,128)} %bitcast.16, s32[2,8,1024]{2,1,0:T(8,128)} %nbr_h.1, ...), custom_call_target="tpu_custom_call" | custom-call | tf_op jit(solution)/shard_map/pallas_call | solution.py:406
  74.5 0.0 copy-start
  74.6 1.4 %copy.21 = f32[2,3,1024]{2,0,1:T(2,128)} copy(f32[2,3,1024]{2,0,1:T(2,128)} %bitcast.14) | data formatting | bytes 49152
  75.9 0.0 copy-done
  75.9 0.0 copy-start.1
  75.9 0.6 copy.22
  76.5 0.1 copy-done.1
  76.6 0.5 copy.23
Async XLA Ops:
  74.5 1.4 %copy-start = (f32[3,2,1024]{2,1,0:T(2,128)S(1)}, f32[3,2,1024]{2,1,0:T(2,128)}, u32[]{:S(2)}) copy-start(f32[3,2,1024]{2,1,0:T(2,128)} %get-tuple-element.7) | copy-start | bytes 73732
  75.9 0.7 copy-start.1

commit v3 on v2

--- a/solution.py
+++ b/solution.py
@@ -12,6 +12,7 @@
 CUTOFF = 5.0
 STEP = 0.2
 LANES = 128
+UNROLL = 4
 MESH = pl.DeviceIdType.MESH
 F32 = jnp.float32
 BF16 = jnp.bfloat16
@@ -69,7 +70,7 @@
     opos, ovel, onw,
     pos, vel, spc, mas, send, nbr, liv, wrad, w1, w2, wup, wout,
     send_pos, halo_pos, send_spc, halo_spc, feat, send_feat, halo_feat, filt2, oh, send_oh,
-    send_lo, low, gath, disp, wbig, sumw, wcat, acc, force, send_frc, recv_frc, every, prod,
+    send_lo, low, gath, disp, wbig, wcat, acc, force, send_frc, recv_frc, every,
     load_sem, send_sem, recv_sem,
 ):
     n_walk, n_dom = lax.axis_size("walker"), lax.axis_size("domain")
@@ -172,12 +173,11 @@
             wbig[:, s * LANES : (s + 1) * LANES] = jnp.concatenate(blocks, axis=0).astype(BF16)
 
     weights_by_slot()
-    for s in range(slots):
-        sumw[s * 2 * LANES : (s + 1) * 2 * LANES, :] = (
-            (lane_iota((2 * LANES, LANES)) == s).astype(F32).astype(BF16)
-        )
-    wcat[:, :LANES] = w1[...]
-    wcat[:, LANES:] = w2[...]
+    wcat[...] = jnp.zeros_like(wcat)
+    for i in range(2):
+        rows = slice(i * LANES, (i + 1) * LANES)
+        wcat[rows, 2 * i * LANES : (2 * i + 1) * LANES] = w1[...]
+        wcat[rows, (2 * i + 1) * LANES : (2 * i + 2) * LANES] = w2[...]
 
     count = wts.shape[1]
     square = (count, count)
@@ -200,28 +200,26 @@
     def build(w, t):
         at = pl.ds(pl.multiple_of(t * LANES, LANES), LANES)
         ids = nbr[w, :, at]
-        key = (ids >> 10) * halo + (ids & (halo - 1))
-        key_t = jnp.transpose(jnp.where(liv[w, :, at] != 0, key, -1))
+        key_t = jnp.transpose(jnp.where(liv[w, :, at] != 0, ids & (halo - 1), -1))
         lo_t = jnp.transpose(ids & (LANES - 1))
         for s in range(slots):
             block = slice(s * LANES, (s + 1) * LANES)
-            oh[w, t, block, :] = one_hot(key_t[:, s : s + 1], 2 * halo)
+            oh[w, t, block, :] = one_hot(key_t[:, s : s + 1], halo)
             low[w, t, block, :] = one_hot(lo_t[:, s : s + 1], LANES)
 
-    def gather_rows(w, t, ids, own, near):
-        second_t = jnp.transpose((ids >> 9) & 1)
-        table = jnp.concatenate(
-            [
-                jnp.concatenate([own[:halo], own[halo:]], axis=1),
-                jnp.concatenate([near[0], near[1]], axis=1),
-            ],
-            axis=0,
-        )
+    def gather_rows(w, t, lane, ids, own, near):
+        odd_t = jnp.transpose((ids >> 9) & 1)
+        far_t = jnp.transpose(ids >> 10)
+        table = jnp.concatenate([own[:halo], own[halo:], near[0], near[1]], axis=1)
         both = dot(oh[w, t], table)
         for s in range(slots):
             block = slice(s * LANES, (s + 1) * LANES)
-            take = jnp.broadcast_to(second_t[:, s : s + 1], (LANES, LANES)) != 0
-            gath[block, :] = jnp.where(take, both[block, LANES:], both[block, :LANES])
+            odd = jnp.broadcast_to(odd_t[:, s : s + 1], (LANES, LANES)) != 0
+            far = jnp.broadcast_to(far_t[:, s : s + 1], (LANES, LANES)) != 0
+            parts = [both[block, i * LANES : (i + 1) * LANES] for i in range(4)]
+            gath[lane, block, :] = jnp.where(
+                far, jnp.where(odd, parts[3], parts[2]), jnp.where(odd, parts[1], parts[0])
+            )
 
     def geometry(w, at, ids):
         hi, lo = ids >> 7, ids & (LANES - 1)
@@ -249,34 +247,43 @@
         turned = jnp.transpose(stacked).astype(BF16)
         return jnp.concatenate([turned, turned], axis=1)
 
-    def first_pass(w, t):
+    def first_gather(w, t, lane):
         at = pl.ds(pl.multiple_of(t * LANES, LANES), LANES)
         ids = nbr[w, :, at]
-        basis = geometry(w, at, ids)
-        gather_rows(w, t, ids, spc[...], halo_spc)
+        gather_rows(w, t, lane, ids, spc[...], halo_spc)
+        return geometry(w, at, ids)
+
+    def first_head(w, t, lane, basis):
+        at = pl.ds(pl.multiple_of(t * LANES, LANES), LANES)
         total = jnp.zeros((LANES, LANES), F32)
-        for s in range(0, slots, 2):
-            hidden = dot(basis, wbig[:, s * LANES : (s + 2) * LANES])
-            radial = silu(hidden).astype(BF16)
-            for i in range(2):
+        for s in range(0, slots, 4):
+            radial = silu(dot(basis, wbig[:, s * LANES : (s + 4) * LANES])).astype(BF16)
+            for i in range(4):
+                if i % 2 == 0:
+                    pair = dot(radial[:, i * LANES : (i + 2) * LANES], wcat[...])
                 block = slice((s + i) * LANES, (s + i + 1) * LANES)
-                filters = dot(radial[:, i * LANES : (i + 1) * LANES], wcat[...])
-                filt2[w, t, block, :] = filters[:, LANES:]
-                total = total + filters[:, :LANES] * gath[block, :]
+                column = (i % 2) * 2 * LANES
+                filt2[w, t, block, :] = pair[:, column + LANES : column + 2 * LANES]
+                total = total + pair[:, column : column + LANES] * gath[lane, block, :]
         updated = dot(total.astype(BF16), wup[...])
         feat[w, at, :] = (spc[at, :].astype(F32) + silu(updated)).astype(BF16)
 
-    def second_pass(w, t):
+    def second_gather(w, t, lane):
         at = pl.ds(pl.multiple_of(t * LANES, LANES), LANES)
         ids = nbr[w, :, at]
-        gather_rows(w, t, ids, feat[w], halo_feat[w])
+        gather_rows(w, t, lane, ids, feat[w], halo_feat[w])
+        return ids
+
+    def second_head(w, t, lane, ids):
+        at = pl.ds(pl.multiple_of(t * LANES, LANES), LANES)
         own = feat[w, at, :].astype(F32) * wout[...]
+        lanes = lane_iota((LANES, LANES))
+        by_slot = jnp.zeros((LANES, LANES), F32)
         for s in range(slots):
             block = slice(s * LANES, (s + 1) * LANES)
-            head, tail = split(filt2[w, t, block, :] * own * gath[block, :])
-            prod[:, 2 * s * LANES : (2 * s + 1) * LANES] = head.astype(BF16)
-            prod[:, (2 * s + 1) * LANES : (2 * s + 2) * LANES] = tail.astype(BF16)
-        coupling = jnp.transpose(dot(prod[...], sumw[...]))[:slots]
+            product = filt2[w, t, block, :] * own * gath[lane, block, :]
+            by_slot = jnp.where(lanes == s, jnp.sum(product, axis=1, keepdims=True), by_slot)
+        coupling = jnp.transpose(by_slot)[:slots]
         hi = ids >> 7
         pieces = []
         for c in range(3):
@@ -298,21 +305,32 @@
             out.append(jnp.concatenate(rows, axis=0).astype(BF16))
         return jnp.concatenate(out, axis=1)
 
-    def loop(body, w):
-        def step(t, carry):
-            body(w, t)
+    def loop(gather, head, w):
+        def step(i, carry):
+            held = gather(w, i * UNROLL, 0)
+            for j in range(UNROLL):
+                later = gather(w, i * UNROLL + j + 1, j + 1) if j + 1 < UNROLL else None
+                head(w, i * UNROLL + j, j, held)
+                held = later
             return carry
 
-        lax.fori_loop(0, groups, step, 0)
-
-    loop(build, 0)
+        lax.fori_loop(0, groups // UNROLL, step, 0)
+
+    def build_all(w):
+        def step(i, carry):
+            for j in range(2):
+                build(w, 2 * i + j)
+            return carry
+
+        lax.fori_loop(0, groups // 2, step, 0)
+
+    for w in range(walkers):
+        build_all(w)
     for copy in moves:
         copy.wait()
     feat_moves = []
     for w in range(walkers):
-        if w:
-            loop(build, w)
-        loop(first_pass, w)
+        loop(first_gather, first_head, w)
         sent = dot(send_oh[...], feat[w]).astype(BF16)
         send_feat[w, 0] = sent[:halo]
         send_feat[w, 1] = sent[halo:]
@@ -324,7 +342,7 @@
         for copy in feat_moves[w]:
             copy.wait()
         acc[...] = jnp.zeros_like(acc)
-        loop(second_pass, w)
+        loop(second_gather, second_head, w)
         reaction = acc[: 3 * high] + acc[3 * high :]
         for c in range(3):
             force[w, c] = force[w, c] - reaction[c * high : c * high + groups]
@@ -433,21 +451,19 @@
             pltpu.VMEM((walkers, *halo_rows), BF16),
             pltpu.VMEM((walkers, *halo_rows), BF16),
             pltpu.VMEM((walkers, groups, edges, channels), F32),
-            pltpu.VMEM((walkers, groups, edges, 2 * halo), BF16),
+            pltpu.VMEM((walkers, groups, edges, halo), BF16),
             pltpu.VMEM((2 * halo, atoms), BF16),
             pltpu.VMEM((2 * halo, LANES), BF16),
             pltpu.VMEM((walkers, groups, edges, LANES), BF16),
-            pltpu.VMEM((edges, channels), F32),
+            pltpu.VMEM((UNROLL, edges, channels), F32),
             pltpu.VMEM((walkers, 3, slots, atoms), F32),
             pltpu.VMEM((4 * orders * slots, slots * channels), BF16),
-            pltpu.VMEM((slots * 2 * channels, LANES), BF16),
-            pltpu.VMEM((channels, 2 * channels), BF16),
+            pltpu.VMEM((2 * channels, 4 * channels), BF16),
             pltpu.VMEM((12 * groups, LANES), F32),
             pltpu.VMEM((walkers, 3, groups, LANES), F32),
             pltpu.VMEM((walkers, 2, 16, LANES), F32),
             pltpu.VMEM((walkers, 2, 16, LANES), F32),
             pltpu.VMEM((n_walk * walkers, 8, atoms), F32),
-            pltpu.VMEM((LANES, slots * 2 * channels), BF16),
             pltpu.SemaphoreType.DMA((12,)),
             pltpu.SemaphoreType.DMA((copies,)),
             pltpu.SemaphoreType.DMA((copies,)),

time: 77.3 us -> 60.2 us (0.78)
  Pallas kernels: 73.9 us -> 56.8 us
    pallas_call x1, Pallas kernels: 73.9 us -> 56.8 us  [on_device(): pl.pallas_call(kernel, out_shape=(jax.ShapeDtypeStruct(by_component, F32)...]
where the time goes in v3:
time: 60.2 us; the launch traced here: 60 us
  Pallas kernels  56.8 us (94%)
  local copies, waits for them, and re-layouts  2.55 us (4%)
  between operations  0.66 us (1%)
    pallas_call x1, Pallas kernels, on_device(): pl.pallas_call(kernel, out_shape=(jax.ShapeDtypeStruct(by_component, F32)...  56.8 us
    unnamed x7, local copies, waits for them, and re-layouts  2.55 us

profile of v3, /device:TPU:0, one launch (start us, length us, event | category | flops | bytes accessed | tf_op | source)
XLA Modules:
  0.0 60.0 jit_solution(7378397610632024219)
XLA Ops:
  0.6 56.8 %shard_map.166 = (f32[3,2,1024]{2,1,0:T(2,128)}, f32[3,2,1024]{2,1,0:T(2,128)}, f32[1,8]{1,0:T(1,128)}) custom-call(f32[3,2,1024]{2,1,0:T(2,128)} %bitcast.11, f32[3,2,1024]{2,1,0:T(2,128)} %bitcast.12, bf16[1024,128]{1,0:T(8,128)(2,1)} %spc_h.1, f32[1,1024]{1,0:T(1,128)} %bitcast.15, s32[1,1024]{1,0:T(1,128)} %bitcast.16, s32[2,8,1024]{2,1,0:T(8,128)} %nbr_h.1, ...), custom_call_target="tpu_custom_call" | custom-call | tf_op jit(solution)/shard_map/pallas_call | solution.py:424
  57.4 0.0 copy-start
  57.4 1.4 %copy.21 = f32[2,3,1024]{2,0,1:T(2,128)} copy(f32[2,3,1024]{2,0,1:T(2,128)} %bitcast.14) | data formatting | bytes 49152
  58.8 0.0 copy-done
  58.8 0.0 copy-start.1
  58.8 0.6 %copy.22 = f32[2,3,1024]{2,0,1:T(2,128)} copy(f32[2,3,1024]{2,0,1:T(2,128)S(1)} %bitcast.13) | data formatting | bytes 49152
  59.4 0.1 copy-done.1
  59.5 0.5 copy.23
Async XLA Ops:
  57.4 1.4 %copy-start = (f32[3,2,1024]{2,1,0:T(2,128)S(1)}, f32[3,2,1024]{2,1,0:T(2,128)}, u32[]{:S(2)}) copy-start(f32[3,2,1024]{2,1,0:T(2,128)} %get-tuple-element.7) | copy-start | bytes 73732
  58.8 0.7 %copy-start.1 = (f32[1,8]{1,0:T(1,128)S(1)}, f32[1,8]{1,0:T(1,128)}, u32[]{:S(2)}) copy-start(f32[1,8]{1,0:T(1,128)} %get-tuple-element.8) | copy-start | bytes 100

commit v4 on v3

--- a/solution.py
+++ b/solution.py
@@ -52,6 +52,13 @@
 
 def dot(a, b):
     return jnp.dot(a, b, preferred_element_type=F32)
+
+
+def choose(both, column):
+    number = jnp.broadcast_to(column, (both.shape[0], LANES))
+    odd, far = (number & 1) != 0, number >= 2
+    parts = [both[:, i * LANES : (i + 1) * LANES] for i in range(4)]
+    return jnp.where(far, jnp.where(odd, parts[3], parts[2]), jnp.where(odd, parts[1], parts[0]))
 
 
 def lane_lookup(rows, hi, lo):
@@ -83,7 +90,9 @@
     slots = nbr.shape[1]
     tile_edges = slots * LANES
     peers = [(me_w, left), (me_w, right)]
-    peers += [(lax.rem(me_w + o, n_walk), me_d) for o in range(1, n_walk)]
+    ranks = [me_w] + [lax.rem(me_w + o, n_walk) for o in range(1, n_walk)]
+    peers += [(rank, me_d) for rank in ranks[1:]]
+    peers += [(rank, side) for rank in ranks[1:] for side in (left, right)]
 
     barrier = pltpu.get_barrier_semaphore()
     for peer in peers:
@@ -143,21 +152,48 @@
             for g in range(groups):
                 q = g % per_side
                 send_pos[g // per_side, row : row + 1, q * LANES : (q + 1) * LANES] = sent[g : g + 1]
-    columns_out = jnp.transpose(rows_out)
-    lo_out = jnp.transpose(out_lo)
+    quarter = atoms // 4
+    columns_out = jnp.transpose(rows_out & (quarter - 1))
+    quarters_out = jnp.transpose(rows_out >> 8)
     for g in range(groups):
         block = slice(g * LANES, (g + 1) * LANES)
-        send_oh[block, :] = one_hot(columns_out[:, g : g + 1], atoms)
-        send_lo[block, :] = one_hot(lo_out[:, g : g + 1], LANES)
+        hot = one_hot(columns_out[:, g : g + 1], quarter)
+        send_oh[block, :] = hot
+        send_lo[block, :] = hot[:, :LANES] + hot[:, LANES:]
+
+    def send_gather(rows, target):
+        table = jnp.concatenate(
+            [rows[i * quarter : (i + 1) * quarter] for i in range(4)], axis=1
+        )
+        both = dot(send_oh[...], table)
+        for g in range(groups):
+            picked = choose(both[g * LANES : (g + 1) * LANES], quarters_out[:, g : g + 1])
+            q = g % per_side
+            target[g // per_side, q * LANES : (q + 1) * LANES, :] = picked.astype(BF16)
+
     loads["spc"].wait()
+    loads["vel"].wait()
+    for w in range(walkers):
+        for c in range(3):
+            every[w, c : c + 1, :] = pos[c, w : w + 1, :]
+            every[w, 3 + c : 4 + c, :] = vel[c, w : w + 1, :]
     pl.semaphore_wait(barrier, len(peers))
     moves = both_ways(send_pos, halo_pos, 0)
-    sent = dot(send_oh[...], spc[...]).astype(BF16)
-    send_spc[0] = sent[:halo]
-    send_spc[1] = sent[halo:]
+    send_gather(spc[...], send_spc)
     moves += both_ways(send_spc, halo_spc, 2)
-
-    for name in ("nbr", "liv", "wrad", "w1", "w2", "wup", "wout", "vel", "mas"):
+    late_moves = []
+    sems = iter(range(4 + 2 * walkers, send_sem.shape[0]))
+
+    def send_late(src, dst, peer):
+        copy = remote(src, dst, next(sems), peer)
+        copy.start()
+        late_moves.append(copy)
+
+    for o in range(1, n_walk):
+        mine, theirs = pl.ds(0, walkers), pl.ds(o * walkers, walkers)
+        send_late(every.at[mine], every.at[theirs], (ranks[o], me_d))
+
+    for name in ("nbr", "liv", "wrad", "w1", "w2", "wup", "wout", "mas"):
         loads[name].wait()
 
     def weights_by_slot():
@@ -201,25 +237,20 @@
         at = pl.ds(pl.multiple_of(t * LANES, LANES), LANES)
         ids = nbr[w, :, at]
         key_t = jnp.transpose(jnp.where(liv[w, :, at] != 0, ids & (halo - 1), -1))
-        lo_t = jnp.transpose(ids & (LANES - 1))
         for s in range(slots):
             block = slice(s * LANES, (s + 1) * LANES)
-            oh[w, t, block, :] = one_hot(key_t[:, s : s + 1], halo)
-            low[w, t, block, :] = one_hot(lo_t[:, s : s + 1], LANES)
+            hot = one_hot(key_t[:, s : s + 1], halo)
+            oh[w, t, block, :] = hot
+            parts = [hot[:, i * LANES : (i + 1) * LANES] for i in range(halo // LANES)]
+            low[w, t, block, :] = functools.reduce(jnp.add, parts)
 
     def gather_rows(w, t, lane, ids, own, near):
-        odd_t = jnp.transpose((ids >> 9) & 1)
-        far_t = jnp.transpose(ids >> 10)
+        quarter_t = jnp.transpose(ids >> 9)
         table = jnp.concatenate([own[:halo], own[halo:], near[0], near[1]], axis=1)
         both = dot(oh[w, t], table)
         for s in range(slots):
             block = slice(s * LANES, (s + 1) * LANES)
-            odd = jnp.broadcast_to(odd_t[:, s : s + 1], (LANES, LANES)) != 0
-            far = jnp.broadcast_to(far_t[:, s : s + 1], (LANES, LANES)) != 0
-            parts = [both[block, i * LANES : (i + 1) * LANES] for i in range(4)]
-            gath[lane, block, :] = jnp.where(
-                far, jnp.where(odd, parts[3], parts[2]), jnp.where(odd, parts[1], parts[0])
-            )
+            gath[lane, block, :] = choose(both[block], quarter_t[:, s : s + 1])
 
     def geometry(w, at, ids):
         hi, lo = ids >> 7, ids & (LANES - 1)
@@ -288,7 +319,7 @@
         pieces = []
         for c in range(3):
             pair = coupling * disp[w, c, :, at]
-            force[w, c, pl.ds(t, 1), :] = jnp.sum(pair, axis=0, keepdims=True)
+            force[w, pl.ds(c * groups + t, 1), :] = jnp.sum(pair, axis=0, keepdims=True)
             pieces.append(split(pair))
         acc[...] += dot(spread_left(pieces, hi, 2 * groups), low[w, t])
 
@@ -331,12 +362,9 @@
     feat_moves = []
     for w in range(walkers):
         loop(first_gather, first_head, w)
-        sent = dot(send_oh[...], feat[w]).astype(BF16)
-        send_feat[w, 0] = sent[:halo]
-        send_feat[w, 1] = sent[halo:]
+        send_gather(feat[w], send_feat.at[w])
         feat_moves.append(both_ways(send_feat.at[w], halo_feat.at[w], 4 + 2 * w))
 
-    force_moves = []
     high = 2 * groups
     for w in range(walkers):
         for copy in feat_moves[w]:
@@ -345,49 +373,41 @@
         loop(second_gather, second_head, w)
         reaction = acc[: 3 * high] + acc[3 * high :]
         for c in range(3):
-            force[w, c] = force[w, c] - reaction[c * high : c * high + groups]
             for side in range(2):
                 start = c * high + groups + side * per_side
                 send_frc[w, side, c * per_side : (c + 1) * per_side, :] = -reaction[
                     start : start + per_side
                 ]
-        base = 4 + 2 * walkers + 2 * w
-        force_moves.append(both_ways(send_frc.at[w], recv_frc.at[w], base))
-
-    state_moves = []
-    for w in range(walkers):
-        for copy in force_moves[w]:
-            copy.wait()
-        pieces = []
-        for c in range(3):
-            rows = slice(c * per_side, (c + 1) * per_side)
-            pieces.append(
-                split(jnp.concatenate([recv_frc[w, 0, rows, :], recv_frc[w, 1, rows, :]], axis=0))
+            force[w, c * groups : (c + 1) * groups, :] = (
+                force[w, c * groups : (c + 1) * groups, :] - reaction[c * high : c * high + groups]
             )
-        back = dot(spread_left(pieces, out_hi, groups), send_lo[...])
-        for c in range(3):
-            total = force[w, c] + (
-                back[c * groups : (c + 1) * groups]
-                + back[(3 + c) * groups : (4 + c) * groups]
-            )
-            flat = jnp.concatenate([total[g : g + 1] for g in range(groups)], axis=1)
-            stepped = vel[c, w : w + 1, :] + STEP * flat / mas[...]
-            every[w, c : c + 1, :] = pos[c, w : w + 1, :] + STEP * stepped
-            every[w, 3 + c : 4 + c, :] = stepped
-        for o in range(1, n_walk):
-            base = 4 + 4 * walkers + w * (n_walk - 1) + o - 1
-            copy = remote(every.at[w], every.at[o * walkers + w], base, peers[1 + o])
-            copy.start()
-            state_moves.append(copy)
-    for copy in state_moves:
+        for o in range(n_walk):
+            slot = o * walkers + w
+            send_late(send_frc.at[w, 0], recv_frc.at[slot, 1], (ranks[o], left))
+            send_late(send_frc.at[w, 1], recv_frc.at[slot, 0], (ranks[o], right))
+            if o:
+                send_late(force.at[w], force.at[slot], (ranks[o], me_d))
+    for copy in late_moves:
         copy.wait()
     for k in range(walkers):
         source = csr_s[me_w * walkers + k]
         behind = lax.rem(me_w - lax.div(source, walkers) + n_walk, n_walk)
-        picked = every[behind * walkers + lax.rem(source, walkers)]
-        for c in range(3):
-            opos[c, k : k + 1, :] = picked[c : c + 1]
-            ovel[c, k : k + 1, :] = picked[3 + c : 4 + c]
+        slot = behind * walkers + lax.rem(source, walkers)
+        state, own, back = every[slot], force[slot], recv_frc[slot]
+        pieces = []
+        for c in range(3):
+            rows = slice(c * per_side, (c + 1) * per_side)
+            pieces.append(split(jnp.concatenate([back[0, rows], back[1, rows]], axis=0)))
+        spread_back = dot(spread_left(pieces, out_hi, groups), send_lo[...])
+        for c in range(3):
+            total = own[c * groups : (c + 1) * groups] + (
+                spread_back[c * groups : (c + 1) * groups]
+                + spread_back[(3 + c) * groups : (4 + c) * groups]
+            )
+            flat = jnp.concatenate([total[g : g + 1] for g in range(groups)], axis=1)
+            stepped = state[3 + c : 4 + c] + STEP * flat / mas[...]
+            opos[c, k : k + 1, :] = state[c : c + 1] + STEP * stepped
+            ovel[c, k : k + 1, :] = stepped
 
 
 def on_device(
@@ -415,7 +435,7 @@
     orders = w_rad.shape[0]
     n_walk = lax.axis_size("walker")
     edges = slots * LANES
-    copies = 4 + 4 * walkers + walkers * (n_walk - 1)
+    copies = 4 + 2 * walkers + (n_walk - 1) + walkers * (3 * n_walk - 1)
     by_component = (3, walkers, atoms)
     hbm = pl.BlockSpec(memory_space=pltpu.HBM)
     vmem = pl.BlockSpec(memory_space=pltpu.VMEM)
@@ -452,7 +472,7 @@
             pltpu.VMEM((walkers, *halo_rows), BF16),
             pltpu.VMEM((walkers, groups, edges, channels), F32),
             pltpu.VMEM((walkers, groups, edges, halo), BF16),
-            pltpu.VMEM((2 * halo, atoms), BF16),
+            pltpu.VMEM((2 * halo, atoms // 4), BF16),
             pltpu.VMEM((2 * halo, LANES), BF16),
             pltpu.VMEM((walkers, groups, edges, LANES), BF16),
             pltpu.VMEM((UNROLL, edges, channels), F32),
@@ -460,9 +480,9 @@
             pltpu.VMEM((4 * orders * slots, slots * channels), BF16),
             pltpu.VMEM((2 * channels, 4 * channels), BF16),
             pltpu.VMEM((12 * groups, LANES), F32),
-            pltpu.VMEM((walkers, 3, groups, LANES), F32),
+            pltpu.VMEM((n_walk * walkers, 3 * groups, LANES), F32),
             pltpu.VMEM((walkers, 2, 16, LANES), F32),
-            pltpu.VMEM((walkers, 2, 16, LANES), F32),
+            pltpu.VMEM((n_walk * walkers, 2, 16, LANES), F32),
             pltpu.VMEM((n_walk * walkers, 8, atoms), F32),
             pltpu.SemaphoreType.DMA((12,)),
             pltpu.SemaphoreType.DMA((copies,)),

time: 60.2 us -> 56.6 us (0.940)
  Pallas kernels: 56.8 us -> 53.2 us
    pallas_call x1, Pallas kernels: 56.8 us -> 53.2 us  [on_device(): pl.pallas_call(kernel, out_shape=(jax.ShapeDtypeStruct(by_component, F32)...]
where the time goes in v4:
time: 56.6 us; the launch traced here: 56.4 us
  Pallas kernels  53.2 us (94%)
  local copies, waits for them, and re-layouts  2.55 us (5%)
  between operations  0.66 us (1%)
    pallas_call x1, Pallas kernels, on_device(): pl.pallas_call(kernel, out_shape=(jax.ShapeDtypeStruct(by_component, F32)...  53.2 us
    unnamed x7, local copies, waits for them, and re-layouts  2.55 us

profile of v4, /device:TPU:0, one launch (start us, length us, event | category | flops | bytes accessed | tf_op | source)
XLA Modules:
  0.0 56.4 jit_solution(5373341093782462295)
XLA Ops:
  0.6 53.2 %shard_map.166 = (f32[3,2,1024]{2,1,0:T(2,128)}, f32[3,2,1024]{2,1,0:T(2,128)}, f32[1,8]{1,0:T(1,128)}) custom-call(f32[3,2,1024]{2,1,0:T(2,128)} %bitcast.11, f32[3,2,1024]{2,1,0:T(2,128)} %bitcast.12, bf16[1024,128]{1,0:T(8,128)(2,1)} %spc_h.1, f32[1,1024]{1,0:T(1,128)} %bitcast.15, s32[1,1024]{1,0:T(1,128)} %bitcast.16, s32[2,8,1024]{2,1,0:T(8,128)} %nbr_h.1, ...), custom_call_target="tpu_custom_call" | custom-call | tf_op jit(solution)/shard_map/pallas_call | solution.py:444
  53.9 0.0 copy-start
  53.9 1.4 %copy.21 = f32[2,3,1024]{2,0,1:T(2,128)} copy(f32[2,3,1024]{2,0,1:T(2,128)} %bitcast.14) | data formatting | bytes 49152
  55.2 0.0 copy-done
  55.2 0.0 copy-start.1
  55.2 0.6 %copy.22 = f32[2,3,1024]{2,0,1:T(2,128)} copy(f32[2,3,1024]{2,0,1:T(2,128)S(1)} %bitcast.13) | data formatting | bytes 49152
  55.9 0.1 copy-done.1
  55.9 0.5 copy.23
Async XLA Ops:
  53.9 1.4 %copy-start = (f32[3,2,1024]{2,1,0:T(2,128)S(1)}, f32[3,2,1024]{2,1,0:T(2,128)}, u32[]{:S(2)}) copy-start(f32[3,2,1024]{2,1,0:T(2,128)} %get-tuple-element.7) | copy-start | bytes 73732
  55.2 0.7 %copy-start.1 = (f32[1,8]{1,0:T(1,128)S(1)}, f32[1,8]{1,0:T(1,128)}, u32[]{:S(2)}) copy-start(f32[1,8]{1,0:T(1,128)} %get-tuple-element.8) | copy-start | bytes 100

commit v5 on v4

--- a/solution.py
+++ b/solution.py
@@ -13,6 +13,8 @@
 STEP = 0.2
 LANES = 128
 UNROLL = 4
+AHEAD = 2
+CHUNK = 4
 MESH = pl.DeviceIdType.MESH
 F32 = jnp.float32
 BF16 = jnp.bfloat16
@@ -77,7 +79,7 @@
     opos, ovel, onw,
     pos, vel, spc, mas, send, nbr, liv, wrad, w1, w2, wup, wout,
     send_pos, halo_pos, send_spc, halo_spc, feat, send_feat, halo_feat, filt2, oh, send_oh,
-    send_lo, low, gath, disp, wbig, wcat, acc, force, send_frc, recv_frc, every,
+    send_lo, low, gath, disp, ext, waves, wbig, wcat, acc, force, send_frc, recv_frc, every,
     load_sem, send_sem, recv_sem,
 ):
     n_walk, n_dom = lax.axis_size("walker"), lax.axis_size("domain")
@@ -244,54 +246,67 @@
             parts = [hot[:, i * LANES : (i + 1) * LANES] for i in range(halo // LANES)]
             low[w, t, block, :] = functools.reduce(jnp.add, parts)
 
-    def gather_rows(w, t, lane, ids, own, near):
+    def gather_rows(w, t, lane, ids, own, near, part=(0, 8)):
         quarter_t = jnp.transpose(ids >> 9)
         table = jnp.concatenate([own[:halo], own[halo:], near[0], near[1]], axis=1)
-        both = dot(oh[w, t], table)
-        for s in range(slots):
+        both = dot(oh[w, t, part[0] * LANES : part[1] * LANES, :], table)
+        for s in range(*part):
             block = slice(s * LANES, (s + 1) * LANES)
-            gath[lane, block, :] = choose(both[block], quarter_t[:, s : s + 1])
+            of = slice((s - part[0]) * LANES, (s - part[0] + 1) * LANES)
+            gath[lane, block, :] = choose(both[of], quarter_t[:, s : s + 1])
 
     def geometry(w, at, ids):
         hi, lo = ids >> 7, ids & (LANES - 1)
         square_sum = None
         for c in range(3):
-            table = [pos[c, w : w + 1, r * LANES : (r + 1) * LANES] for r in range(groups)]
-            for side in range(2):
-                shift = 0.0 if c else (OFFSET if side else -OFFSET)
-                for q in range(per_side):
-                    row = w * 3 + c
-                    table.append(
-                        halo_pos[side, row : row + 1, q * LANES : (q + 1) * LANES] + shift
-                    )
-            delta = lane_lookup(table, hi, lo) - pos[c, w : w + 1, at]
+            table = [ext[w, c, r : r + 1, :] for r in range(2 * groups)]
+            delta = lane_lookup(table, hi, lo) - every[w, c : c + 1, at]
             disp[w, c, :, at] = delta
             square_sum = delta * delta if c == 0 else square_sum + delta * delta
         scaled = jnp.sqrt(square_sum) / CUTOFF
         envelope = jnp.square(jnp.maximum(0.0, 1.0 - scaled * scaled))
         first = jnp.cos(jnp.minimum(scaled, 1.0) * math.pi)
-        waves = [first, 2.0 * first * first - 1.0]
-        while len(waves) < wrad.shape[0]:
-            waves.append(2.0 * first * waves[-1] - waves[-2])
-        pieces = [split(wave * envelope) for wave in waves]
+        cosines = [first, 2.0 * first * first - 1.0]
+        while len(cosines) < wrad.shape[0]:
+            cosines.append(2.0 * first * cosines[-1] - cosines[-2])
+        pieces = [split(wave * envelope) for wave in cosines]
         stacked = jnp.concatenate([p[0] for p in pieces] + [p[1] for p in pieces], axis=0)
-        turned = jnp.transpose(stacked).astype(BF16)
-        return jnp.concatenate([turned, turned], axis=1)
-
-    def first_gather(w, t, lane):
+        return jnp.transpose(stacked).astype(BF16)
+
+    def tile_of(number):
+        if isinstance(number, int):
+            return divmod(number, groups)
+        return lax.div(number, groups), lax.rem(number, groups)
+
+    def first_gather(number, lane, part):
+        w, t = tile_of(number)
         at = pl.ds(pl.multiple_of(t * LANES, LANES), LANES)
         ids = nbr[w, :, at]
-        gather_rows(w, t, lane, ids, spc[...], halo_spc)
-        return geometry(w, at, ids)
-
-    def first_head(w, t, lane, basis):
+        gather_rows(w, t, lane, ids, spc[...], halo_spc, part)
+
+    def first_waves(number, lane):
+        w, t = tile_of(number)
         at = pl.ds(pl.multiple_of(t * LANES, LANES), LANES)
+        waves[lane] = geometry(w, at, nbr[w, :, at])
+
+    def first_head(number, lane, ahead, ahead_lane):
+        w, t = tile_of(number)
+        at = pl.ds(pl.multiple_of(t * LANES, LANES), LANES)
+        basis = jnp.concatenate([waves[lane], waves[lane]], axis=1)
+        first_waves(ahead, ahead_lane)
         total = jnp.zeros((LANES, LANES), F32)
         for s in range(0, slots, 4):
-            radial = silu(dot(basis, wbig[:, s * LANES : (s + 4) * LANES])).astype(BF16)
+            hidden = dot(basis, wbig[:, s * LANES : (s + 4) * LANES])
+            if CHUNK == 2:
+                first_gather(ahead, ahead_lane, (s, s + 2))
+            else:
+                first_gather(ahead, ahead_lane, (s, s + 4))
+            radial = silu(hidden).astype(BF16)
             for i in range(4):
                 if i % 2 == 0:
                     pair = dot(radial[:, i * LANES : (i + 2) * LANES], wcat[...])
+                    if i == 0 and CHUNK == 2:
+                        first_gather(ahead, ahead_lane, (s + 2, s + 4))
                 block = slice((s + i) * LANES, (s + i + 1) * LANES)
                 column = (i % 2) * 2 * LANES
                 filt2[w, t, block, :] = pair[:, column + LANES : column + 2 * LANES]
@@ -347,6 +362,18 @@
 
         lax.fori_loop(0, groups // UNROLL, step, 0)
 
+    def first_loop(w):
+        last = walkers * groups - 1
+
+        def step(i, carry):
+            number = w * groups + i * AHEAD
+            for j in range(AHEAD):
+                ahead = jnp.minimum(number + j + 1, last)
+                first_head(number + j, j % 2, ahead, (j + 1) % 2)
+            return carry
+
+        lax.fori_loop(0, groups // AHEAD, step, 0)
+
     def build_all(w):
         def step(i, carry):
             for j in range(2):
@@ -359,9 +386,23 @@
         build_all(w)
     for copy in moves:
         copy.wait()
+    for w in range(walkers):
+        for c in range(3):
+            row = w * 3 + c
+            for g in range(groups):
+                block = slice(g * LANES, (g + 1) * LANES)
+                ext[w, c, g : g + 1, :] = pos[c, w : w + 1, block]
+                side, q = g // per_side, g % per_side
+                shift = 0.0 if c else (OFFSET if side else -OFFSET)
+                block = slice(q * LANES, (q + 1) * LANES)
+                ext[w, c, groups + g : groups + g + 1, :] = (
+                    halo_pos[side, row : row + 1, block] + shift
+                )
+    first_waves(0, 0)
+    first_gather(0, 0, (0, slots))
     feat_moves = []
     for w in range(walkers):
-        loop(first_gather, first_head, w)
+        first_loop(w)
         send_gather(feat[w], send_feat.at[w])
         feat_moves.append(both_ways(send_feat.at[w], halo_feat.at[w], 4 + 2 * w))
 
@@ -477,6 +518,8 @@
             pltpu.VMEM((walkers, groups, edges, LANES), BF16),
             pltpu.VMEM((UNROLL, edges, channels), F32),
             pltpu.VMEM((walkers, 3, slots, atoms), F32),
+            pltpu.VMEM((walkers, 3, 2 * groups, LANES), F32),
+            pltpu.VMEM((2, LANES, 2 * orders * slots), BF16),
             pltpu.VMEM((4 * orders * slots, slots * channels), BF16),
             pltpu.VMEM((2 * channels, 4 * channels), BF16),
             pltpu.VMEM((12 * groups, LANES), F32),

time: 56.6 us -> 54.9 us (0.970)
  Pallas kernels: 53.2 us -> 51.5 us
    pallas_call x1, Pallas kernels: 53.2 us -> 51.5 us  [on_device(): pl.pallas_call(kernel, out_shape=(jax.ShapeDtypeStruct(by_component, F32)...]
where the time goes in v5:
time: 54.9 us; the launch traced here: 54.7 us
  Pallas kernels  51.5 us (94%)
  local copies, waits for them, and re-layouts  2.55 us (5%)
  between operations  0.66 us (1%)
    pallas_call x1, Pallas kernels, on_device(): pl.pallas_call(kernel, out_shape=(jax.ShapeDtypeStruct(by_component, F32)...  51.5 us
    unnamed x7, local copies, waits for them, and re-layouts  2.55 us

profile of v5, /device:TPU:0, one launch (start us, length us, event | category | flops | bytes accessed | tf_op | source)
XLA Modules:
  0.0 54.7 jit_solution(2944096459575314180)
XLA Ops:
  0.6 51.5 %shard_map.166 = (f32[3,2,1024]{2,1,0:T(2,128)}, f32[3,2,1024]{2,1,0:T(2,128)}, f32[1,8]{1,0:T(1,128)}) custom-call(f32[3,2,1024]{2,1,0:T(2,128)} %bitcast.11, f32[3,2,1024]{2,1,0:T(2,128)} %bitcast.12, bf16[1024,128]{1,0:T(8,128)(2,1)} %spc_h.1, f32[1,1024]{1,0:T(1,128)} %bitcast.15, s32[1,1024]{1,0:T(1,128)} %bitcast.16, s32[2,8,1024]{2,1,0:T(8,128)} %nbr_h.1, ...), custom_call_target="tpu_custom_call" | custom-call | tf_op jit(solution)/shard_map/pallas_call | solution.py:485
  52.2 0.0 copy-start
  52.2 1.4 %copy.21 = f32[2,3,1024]{2,0,1:T(2,128)} copy(f32[2,3,1024]{2,0,1:T(2,128)} %bitcast.14) | data formatting | bytes 49152
  53.5 0.0 copy-done
  53.5 0.0 copy-start.1
  53.5 0.6 %copy.22 = f32[2,3,1024]{2,0,1:T(2,128)} copy(f32[2,3,1024]{2,0,1:T(2,128)S(1)} %bitcast.13) | data formatting | bytes 49152
  54.1 0.1 copy-done.1
  54.2 0.5 copy.23
Async XLA Ops:
  52.2 1.4 %copy-start = (f32[3,2,1024]{2,1,0:T(2,128)S(1)}, f32[3,2,1024]{2,1,0:T(2,128)}, u32[]{:S(2)}) copy-start(f32[3,2,1024]{2,1,0:T(2,128)} %get-tuple-element.7) | copy-start | bytes 73732
  53.5 0.7 %copy-start.1 = (f32[1,8]{1,0:T(1,128)S(1)}, f32[1,8]{1,0:T(1,128)}, u32[]{:S(2)}) copy-start(f32[1,8]{1,0:T(1,128)} %get-tuple-element.8) | copy-start | bytes 100

commit v6 on v5

--- a/solution.py
+++ b/solution.py
@@ -12,9 +12,8 @@
 CUTOFF = 5.0
 STEP = 0.2
 LANES = 128
-UNROLL = 4
+UNROLL = 8
 AHEAD = 2
-CHUNK = 4
 MESH = pl.DeviceIdType.MESH
 F32 = jnp.float32
 BF16 = jnp.bfloat16
@@ -297,20 +296,16 @@
         total = jnp.zeros((LANES, LANES), F32)
         for s in range(0, slots, 4):
             hidden = dot(basis, wbig[:, s * LANES : (s + 4) * LANES])
-            if CHUNK == 2:
-                first_gather(ahead, ahead_lane, (s, s + 2))
-            else:
-                first_gather(ahead, ahead_lane, (s, s + 4))
+            first_gather(ahead, ahead_lane, (0, 3) if s == 0 else (3, 6))
             radial = silu(hidden).astype(BF16)
             for i in range(4):
                 if i % 2 == 0:
                     pair = dot(radial[:, i * LANES : (i + 2) * LANES], wcat[...])
-                    if i == 0 and CHUNK == 2:
-                        first_gather(ahead, ahead_lane, (s + 2, s + 4))
                 block = slice((s + i) * LANES, (s + i + 1) * LANES)
                 column = (i % 2) * 2 * LANES
                 filt2[w, t, block, :] = pair[:, column + LANES : column + 2 * LANES]
                 total = total + pair[:, column : column + LANES] * gath[lane, block, :]
+        first_gather(ahead, ahead_lane, (6, slots))
         updated = dot(total.astype(BF16), wup[...])
         feat[w, at, :] = (spc[at, :].astype(F32) + silu(updated)).astype(BF16)
 

time: 54.9 us -> 54.2 us (0.987)
  Pallas kernels: 51.5 us -> 50.8 us
    pallas_call x1, Pallas kernels: 51.5 us -> 50.8 us  [on_device(): pl.pallas_call(kernel, out_shape=(jax.ShapeDtypeStruct(by_component, F32)...]
where the time goes in v6:
time: 54.2 us; the launch traced here: 54 us
  Pallas kernels  50.8 us (94%)
  local copies, waits for them, and re-layouts  2.55 us (5%)
  between operations  0.66 us (1%)
    pallas_call x1, Pallas kernels, on_device(): pl.pallas_call(kernel, out_shape=(jax.ShapeDtypeStruct(by_component, F32)...  50.8 us
    unnamed x7, local copies, waits for them, and re-layouts  2.55 us

profile of v6, /device:TPU:0, one launch (start us, length us, event | category | flops | bytes accessed | tf_op | source)
XLA Modules:
  0.0 54.0 jit_solution(8038364864894287835)
XLA Ops:
  0.6 50.8 %shard_map.166 = (f32[3,2,1024]{2,1,0:T(2,128)}, f32[3,2,1024]{2,1,0:T(2,128)}, f32[1,8]{1,0:T(1,128)}) custom-call(f32[3,2,1024]{2,1,0:T(2,128)} %bitcast.11, f32[3,2,1024]{2,1,0:T(2,128)} %bitcast.12, bf16[1024,128]{1,0:T(8,128)(2,1)} %spc_h.1, f32[1,1024]{1,0:T(1,128)} %bitcast.15, s32[1,1024]{1,0:T(1,128)} %bitcast.16, s32[2,8,1024]{2,1,0:T(8,128)} %nbr_h.1, ...), custom_call_target="tpu_custom_call" | custom-call | tf_op jit(solution)/shard_map/pallas_call | solution.py:480
  51.4 0.0 copy-start
  51.5 1.4 %copy.21 = f32[2,3,1024]{2,0,1:T(2,128)} copy(f32[2,3,1024]{2,0,1:T(2,128)} %bitcast.14) | data formatting | bytes 49152
  52.8 0.0 copy-done
  52.8 0.0 copy-start.1
  52.8 0.6 %copy.22 = f32[2,3,1024]{2,0,1:T(2,128)} copy(f32[2,3,1024]{2,0,1:T(2,128)S(1)} %bitcast.13) | data formatting | bytes 49152
  53.4 0.1 copy-done.1
  53.5 0.5 copy.23
Async XLA Ops:
  51.4 1.4 %copy-start = (f32[3,2,1024]{2,1,0:T(2,128)S(1)}, f32[3,2,1024]{2,1,0:T(2,128)}, u32[]{:S(2)}) copy-start(f32[3,2,1024]{2,1,0:T(2,128)} %get-tuple-element.7) | copy-start | bytes 73732
  52.8 0.7 %copy-start.1 = (f32[1,8]{1,0:T(1,128)S(1)}, f32[1,8]{1,0:T(1,128)}, u32[]{:S(2)}) copy-start(f32[1,8]{1,0:T(1,128)} %get-tuple-element.8) | copy-start | bytes 100
